TPU v7x, 32 devices: a whole 2x2x4 slice. The times are simulated.
32 devices in a mesh: dp: 2 (over core), seq: 16 (over z, y, x).
Axes of the slice: x: 2, y: 2, z: 4, core: 2. Of those that a mesh axis runs over, the one named last changes fastest.
Arguments:
- block_input: bfloat16 [8192, 1024], P(('dp', 'seq')), may hold values from -6 to 6
- lengths: int32 [2, 2], P('dp'), may hold values from 1 to 1537, 2050 in all within a row
- attn_gain: float32 [1024], replicated, may hold values from 0.5 to 1.5
- w_query: bfloat16 [1024, 1024], replicated, may hold values from -0.1875 to 0.1875
- w_key: bfloat16 [1024, 2048], replicated, may hold values from -0.1875 to 0.1875
- w_value: bfloat16 [1024, 2048], replicated, may hold values from -0.1875 to 0.1875
- w_outgate: bfloat16 [1024, 1024], replicated, may hold values from -0.1875 to 0.1875
- w_beta: bfloat16 [1024, 16], replicated, may hold values from -0.1875 to 0.1875
- w_decay: bfloat16 [1024, 8], replicated, may hold values from -0.1875 to 0.1875
- beta_bias: float32 [16], replicated, may hold values from -3 to 1
- decay_rate: float32 [8], replicated, may hold values from 0.0002 to 0.05
- conv_query: float32 [4, 1024], replicated, may hold values from -3 to 3
- conv_key: float32 [4, 2048], replicated, may hold values from -3 to 3
- conv_value: float32 [4, 2048], replicated, may hold values from -3 to 3
- out_gain: float32 [128], replicated, may hold values from 0.5 to 1.5
- w_out: bfloat16 [1024, 1024], replicated, may hold values from -0.1875 to 0.1875
- mlp_gain: float32 [1024], replicated, may hold values from 0.5 to 1.5
- w_gate: bfloat16 [1024, 2816], replicated, may hold values from -0.1875 to 0.1875
- w_up: bfloat16 [1024, 2816], replicated, may hold values from -0.1875 to 0.1875
- w_down: bfloat16 [2816, 1024], replicated, may hold values from -0.109375 to 0.109375
- out_grad: bfloat16 [8192, 1024], P(('dp', 'seq')), may hold values from -6 to 6
Outputs:
- block_output: bfloat16 [8192, 1024], P(('dp', 'seq'))
- input_grad: bfloat16 [8192, 1024], P(('dp', 'seq'))
- grad_attn_gain: float32 [1024], P(('dp', 'seq'))
- grad_w_query: float32 [1024, 1024], P(('dp', 'seq'))
- grad_w_key: float32 [1024, 2048], P(('dp', 'seq'))
- grad_w_value: float32 [1024, 2048], P(('dp', 'seq'))
- grad_w_outgate: float32 [1024, 1024], P(('dp', 'seq'))
- grad_w_beta: float32 [1024, 16], P(('dp', 'seq'))
- grad_w_decay: float32 [1024, 8], P(('dp', 'seq'))
- grad_beta_bias: float32 [16], replicated
- grad_decay_rate: float32 [8], replicated
- grad_conv_query: float32 [4, 1024], replicated
- grad_conv_key: float32 [4, 2048], replicated
- grad_conv_value: float32 [4, 2048], replicated
- grad_out_gain: float32 [128], replicated
- grad_w_out: float32 [1024, 1024], P(None, ('dp', 'seq'))
- grad_mlp_gain: float32 [1024], P(('dp', 'seq'))
- grad_w_gate: float32 [1024, 2816], P(('dp', 'seq'))
- grad_w_up: float32 [1024, 2816], P(('dp', 'seq'))
- grad_w_down: float32 [2816, 1024], P(None, ('dp', 'seq'))
Inputs may be any that keep to these rules, and one draw needn't show every extreme that they name: `lengths`: row r lists the 2 sequences of group r in packing order; the longest is at most 2560 tokens and every row sums to 2050.
All inputs are finite; a program needn't handle non-finite values.
Results may differ from a plain program's by a relative error of at most 0.022.
Values may be sent and summed in bfloat16 or wider, within the bound.
A program may use at most 512 MiB of HBM per device.

v0:
```python
from functools import partial

import jax
import jax.numpy as jnp
from jax import lax
from jax.sharding import PartitionSpec as P

REFLECTS = 2
KW = 4
BLOCK = 64
SHORTEST = 1024


EXACT_PRECISION = lax.Precision.HIGHEST
RESET_LOG = -80.0


def passed_along(block, axis, distance):
    devices = range(lax.axis_size(axis))
    route = [(i - distance, i) for i in devices if i - distance in devices]
    return lax.ppermute(block, axis, route)


def prefix_2(value, axis, join, neutral):
    place = lax.axis_index(axis)
    gathered = jax.tree.map(
        lambda a, kind: lax.all_gather(a.astype(kind), axis), value, (jnp.bfloat16, jnp.bfloat16)
    )
    state = jax.tree.map(lambda a, e: jnp.zeros_like(a) + jnp.asarray(e, a.dtype), value, neutral)

    def one(lap, state):
        return join(
            state,
            jax.tree.map(
                lambda a, own: lax.dynamic_index_in_dim(a, lap, 0, False).astype(own.dtype),
                gathered,
                value,
            ),
        )

    return lax.fori_loop(0, place, one, state)


def prefix_3(value, axis, join, neutral):
    count, mine = (lax.axis_size(axis), lax.axis_index(axis))
    pieces = jax.tree.map(lambda part: lax.all_gather(part, axis), value)
    pieces = jax.tree.map(lambda part: part[::-1], pieces)
    mine = count - 1 - mine
    so_far = jax.tree.map(
        lambda part, zero: jnp.full_like(part, 0) + jnp.asarray(zero, part.dtype), value, neutral
    )

    def lap(position, so_far):
        longer = join(so_far, jax.tree.map(lambda part: part[position], pieces))
        return jax.tree.map(lambda new, old: jnp.where(position < mine, new, old), longer, so_far)

    return lax.fori_loop(0, count - 1, lap, so_far)


def rms_scale(field, gain, epsilon):
    return field * lax.rsqrt(jnp.mean(field * field, axis=-1, keepdims=True) + epsilon) * gain


def low_round(field):
    return lax.optimization_barrier(field.astype(jnp.bfloat16)).astype(jnp.float32)


def contract_rows(first_op, second_op):
    return lax.dot_general(
        first_op, second_op, (((0,), (0,)), ((), ())), preferred_element_type=jnp.float32
    )


def contract_cols(first_op, second_op):
    return lax.dot_general(
        first_op, second_op, (((1,), (1,)), ((), ())), preferred_element_type=jnp.float32
    )


def compose_maps(earlier, later):
    return (
        jnp.einsum("hij,hjk->hik", later[0], earlier[0], precision=EXACT_PRECISION),
        jnp.einsum("hij,hjk->hik", later[0], earlier[1], precision=EXACT_PRECISION) + later[1],
    )


def seq_positions(extras, first, total_rows):
    sizes = extras + (SHORTEST - 1)
    ends = jnp.cumsum(sizes)
    starts = ends - sizes
    row_ids = first + jnp.arange(total_rows, dtype=jnp.int32)
    inside = (row_ids[:, None] >= starts[None, :]) & (row_ids[:, None] < ends[None, :])
    return row_ids - jnp.sum(jnp.where(inside, starts[None, :], 0), axis=1)


def short_conv(padded, taps, places):
    total_rows = places.shape[0]
    result = jnp.zeros((total_rows, padded.shape[1]), jnp.float32)
    for offset in range(KW):
        back_steps = KW - 1 - offset
        live_rows = (places >= back_steps).astype(jnp.float32)[:, None]
        result = result + taps[offset] * padded[offset : offset + total_rows] * live_rows
    return result


def features(
    places,
    ext_query,
    ext_key,
    ext_value,
    conv_query,
    conv_key,
    conv_value,
    beta_in,
    decay_in,
    beta_bias,
    decay_rate,
):
    total_rows = places.shape[0]
    head_count = decay_in.shape[1]
    queries = jax.nn.silu(short_conv(ext_query, conv_query, places)).reshape(
        total_rows, head_count, -1
    )
    every_key_row = jax.nn.silu(short_conv(ext_key, conv_key, places)).reshape(
        total_rows, head_count, REFLECTS, -1
    )
    values_all = jax.nn.silu(short_conv(ext_value, conv_value, places)).reshape(
        total_rows, head_count, REFLECTS, -1
    )
    head_width = queries.shape[-1]
    queries = (
        queries
        * lax.rsqrt(jnp.sum(queries * queries, axis=-1, keepdims=True) + 1e-06)
        * head_width ** (-0.5)
    )
    every_key_row = every_key_row * lax.rsqrt(
        jnp.sum(every_key_row * every_key_row, axis=-1, keepdims=True) + 1e-06
    )
    betas = jax.nn.sigmoid(beta_in + beta_bias).reshape(total_rows, head_count, REFLECTS)
    log_rate = -decay_rate * jax.nn.softplus(decay_in)
    log_rate = jnp.where((places == 0)[:, None], RESET_LOG, log_rate)
    log_steps = jnp.concatenate(
        [log_rate[:, :, None], jnp.zeros((total_rows, head_count, REFLECTS - 1), jnp.float32)],
        axis=-1,
    )
    return (queries, every_key_row, values_all, betas, log_steps)


def step_layout(field, blocks):
    head_count = field.shape[1]
    moved = field.reshape((blocks, BLOCK) + field.shape[1:])
    moved = jnp.moveaxis(moved, 2, 1)
    return moved.reshape((blocks, head_count, BLOCK * REFLECTS) + field.shape[3:])


def mixer_local(queries, every_key_row, values_all, betas, log_steps):
    rows_here, head_count, head_width = queries.shape
    blocks = rows_here // BLOCK
    steps = BLOCK * REFLECTS
    q_blocks = queries.reshape(blocks, BLOCK, head_count, head_width).transpose(0, 2, 1, 3)
    k_blocks = step_layout(every_key_row, blocks)
    v_blocks = step_layout(values_all, blocks)
    b_blocks = step_layout(betas, blocks)
    cumul = jnp.cumsum(step_layout(log_steps, blocks), axis=-1)
    index = jnp.arange(steps)
    lower_mask = index[:, None] >= index[None, :]
    strict_mask = index[:, None] > index[None, :]
    fading = jnp.exp(jnp.where(lower_mask, cumul[..., :, None] - cumul[..., None, :], -jnp.inf))
    key_inner_products = jnp.einsum(
        "bhmd,bhnd->bhmn", k_blocks, k_blocks, precision=EXACT_PRECISION
    )
    system = (
        jnp.eye(steps, dtype=jnp.float32)
        + jnp.where(strict_mask, fading * key_inner_products, 0.0) * b_blocks[..., :, None]
    )
    growth = jnp.exp(cumul)
    rhs = jnp.concatenate(
        [b_blocks[..., None] * v_blocks, (b_blocks * growth)[..., None] * k_blocks], axis=-1
    )
    solved = jax.scipy.linalg.solve_triangular(system, rhs, lower=True, unit_diagonal=True)
    update = solved[..., :head_width]
    weight_rows = solved[..., head_width:]
    query_fade = fading[..., REFLECTS - 1 :: REFLECTS, :] * jnp.einsum(
        "bhtd,bhnd->bhtn", q_blocks, k_blocks, precision=EXACT_PRECISION
    )
    local_out = jnp.einsum("bhtn,bhne->bhte", query_fade, update, precision=EXACT_PRECISION)
    carry_q = growth[..., REFLECTS - 1 :: REFLECTS, None] * q_blocks - jnp.einsum(
        "bhtn,bhnd->bhtd", query_fade, weight_rows, precision=EXACT_PRECISION
    )
    tail_keys = jnp.exp(cumul[..., -1:] - cumul)[..., None] * k_blocks
    identity_map = jnp.eye(head_width, dtype=jnp.float32)
    transit = jnp.exp(cumul[..., -1])[..., None, None] * identity_map - jnp.einsum(
        "bhnd,bhne->bhde", tail_keys, weight_rows, precision=EXACT_PRECISION
    )
    offsets = jnp.einsum("bhnd,bhne->bhde", tail_keys, update, precision=EXACT_PRECISION)

    def advance(carry, parts):
        return (compose_maps(carry, parts), carry)

    start = (
        jnp.broadcast_to(identity_map, (head_count, head_width, head_width)),
        jnp.zeros((head_count, head_width, head_width), jnp.float32),
    )
    final_maps, prefix = lax.scan(advance, start, (transit, offsets))
    local_out = local_out + jnp.einsum(
        "bhtd,bhde->bhte", carry_q, prefix[1], precision=EXACT_PRECISION
    )
    query_row_total = jnp.einsum("bhtd,bhde->bhte", carry_q, prefix[0], precision=EXACT_PRECISION)
    return (local_out, query_row_total, final_maps[0], final_maps[1])


def gated_output(attended, gate_in, out_gain):
    rows_here, head_count, head_width = attended.shape
    normed = rms_scale(attended, out_gain, 1e-05) * jax.nn.silu(gate_in.reshape(attended.shape))
    return normed.reshape(rows_here, head_count * head_width)


def settle(grad_ext, rim_grad, rim_rows):
    inner_part = grad_ext[rim_rows:]
    keep_part = inner_part[: inner_part.shape[0] - rim_rows]
    last_part = inner_part[inner_part.shape[0] - rim_rows :] + rim_grad
    return jnp.concatenate([keep_part, last_part], axis=0)


def split_columns(matrix, widths):
    pieces = []
    begin = 0
    for width in widths:
        pieces.append(matrix[:, begin : begin + width])
        begin = begin + width
    return pieces


def per_device(
    block_input,
    lengths,
    attn_gain,
    w_query,
    w_key,
    w_value,
    w_outgate,
    w_beta,
    w_decay,
    beta_bias,
    decay_rate,
    conv_query,
    conv_key,
    conv_value,
    out_gain,
    w_out,
    mlp_gain,
    w_gate,
    w_up,
    w_down,
    out_grad,
):
    rows_here = block_input.shape[0]
    rim_rows = KW - 1
    places = seq_positions(lengths[0], lax.axis_index("seq") * rows_here, rows_here)
    xf = block_input.astype(jnp.float32)
    normed, norm_pull = jax.vjp(lambda field, gain: rms_scale(field, gain, 1e-06), xf, attn_gain)
    normed_b = normed.astype(jnp.bfloat16)

    def project(matrix):
        return jnp.dot(normed_b, matrix, preferred_element_type=jnp.float32)

    q_pre = project(w_query).astype(jnp.bfloat16)
    k_pre = project(w_key).astype(jnp.bfloat16)
    v_pre = project(w_value).astype(jnp.bfloat16)
    gate_pre = project(w_outgate)
    beta_pre = project(w_beta)
    decay_pre = project(w_decay)
    received = passed_along(
        (
            q_pre[rows_here - rim_rows :],
            k_pre[rows_here - rim_rows :],
            v_pre[rows_here - rim_rows :],
        ),
        "seq",
        1,
    )
    ext_query = jnp.concatenate([received[0], q_pre], axis=0).astype(jnp.float32)
    ext_key = jnp.concatenate([received[1], k_pre], axis=0).astype(jnp.float32)
    ext_value = jnp.concatenate([received[2], v_pre], axis=0).astype(jnp.float32)
    featured, feat_pull = jax.vjp(
        partial(features, places),
        ext_query,
        ext_key,
        ext_value,
        conv_query,
        conv_key,
        conv_value,
        beta_pre,
        decay_pre,
        beta_bias,
        decay_rate,
    )
    mixer_in = (
        low_round(featured[0]),
        low_round(featured[1]),
        low_round(featured[2]),
        featured[3],
        featured[4],
    )
    mixed, mixer_pull = jax.vjp(mixer_local, *mixer_in)
    local_out, query_row_total, state_map, state_add = mixed
    head_count = state_map.shape[0]
    head_width = state_map.shape[1]
    blocks = local_out.shape[0]
    identity_map = jnp.broadcast_to(jnp.eye(head_width, dtype=jnp.float32), state_map.shape)
    zero_maps = jnp.zeros(state_map.shape, jnp.float32)
    start_state = prefix_2((state_map, state_add), "seq", compose_maps, (identity_map, zero_maps))[
        1
    ]
    block_out = local_out + jnp.einsum(
        "bhtd,hde->bhte", query_row_total, start_state, precision=EXACT_PRECISION
    )
    attended = block_out.transpose(0, 2, 1, 3).reshape(rows_here, head_count, head_width)
    gated, gate_pull = jax.vjp(gated_output, attended, gate_pre, out_gain)
    gated_b = gated.astype(jnp.bfloat16)
    resid = xf + jnp.dot(gated_b, w_out, preferred_element_type=jnp.float32)
    mlp_in, mlp_pull = jax.vjp(lambda field, gain: rms_scale(field, gain, 1e-06), resid, mlp_gain)
    mlp_b = mlp_in.astype(jnp.bfloat16)
    gate_act = jnp.dot(mlp_b, w_gate, preferred_element_type=jnp.float32)
    up_act = jnp.dot(mlp_b, w_up, preferred_element_type=jnp.float32)
    hidden, act_pull = jax.vjp(
        lambda first_op, second_op: jax.nn.silu(first_op) * second_op, gate_act, up_act
    )
    hidden_b = hidden.astype(jnp.bfloat16)
    block_output = (resid + jnp.dot(hidden_b, w_down, preferred_element_type=jnp.float32)).astype(
        jnp.bfloat16
    )
    d_hidden = contract_cols(out_grad, w_down)
    gate_cotangent, d_up = act_pull(d_hidden)
    d_gate_b = gate_cotangent.astype(jnp.bfloat16)
    d_up_b = d_up.astype(jnp.bfloat16)
    d_mlp = contract_cols(d_gate_b, w_gate) + contract_cols(d_up_b, w_up)
    d_resid_mlp, grad_mlp_gain = mlp_pull(d_mlp)
    d_resid = out_grad.astype(jnp.float32) + d_resid_mlp
    d_branch_b = d_resid.astype(jnp.bfloat16)
    d_gated = contract_cols(d_branch_b, w_out)
    branch_widths = [w_out.shape[0], w_gate.shape[1], w_up.shape[1], w_down.shape[0], 1]
    d_attended, d_gate_pre, grad_out_gain = gate_pull(d_gated)
    d_block = d_attended.reshape(blocks, BLOCK, head_count, head_width).transpose(0, 2, 1, 3)
    state_part = jnp.einsum("bhtd,bhte->hde", query_row_total, d_block, precision=EXACT_PRECISION)
    after_grad = prefix_3(
        (state_map.transpose(0, 2, 1), state_part), "seq", compose_maps, (identity_map, zero_maps)
    )[1]
    cotangent = (
        d_block,
        jnp.einsum("bhte,hde->bhtd", d_block, start_state, precision=EXACT_PRECISION),
        jnp.einsum("hde,hfe->hdf", after_grad, start_state, precision=EXACT_PRECISION),
        after_grad,
    )
    d_featured = mixer_pull(cotangent)
    (
        d_ext_query,
        d_ext_key,
        d_ext_value,
        grad_conv_query,
        grad_conv_key,
        grad_conv_value,
        d_beta_pre,
        d_decay_pre,
        grad_beta_bias,
        grad_decay_rate,
    ) = feat_pull(d_featured)
    rim_back = (
        passed_along(d_ext_query[:rim_rows].astype(jnp.bfloat16), "seq", -1).astype(jnp.float32),
        passed_along(d_ext_key[:rim_rows].astype(jnp.bfloat16), "seq", -1).astype(jnp.float32),
        passed_along(d_ext_value[:rim_rows].astype(jnp.bfloat16), "seq", -1).astype(jnp.float32),
    )
    d_query_b = settle(d_ext_query, rim_back[0], rim_rows).astype(jnp.bfloat16)
    key_block_cotangent = settle(d_ext_key, rim_back[1], rim_rows).astype(jnp.bfloat16)
    d_value_b = settle(d_ext_value, rim_back[2], rim_rows).astype(jnp.bfloat16)
    d_outgate_b = d_gate_pre.astype(jnp.bfloat16)
    d_beta_b = d_beta_pre.astype(jnp.bfloat16)
    d_decay_b = d_decay_pre.astype(jnp.bfloat16)
    d_normed = (
        contract_cols(d_query_b, w_query)
        + contract_cols(key_block_cotangent, w_key)
        + contract_cols(d_value_b, w_value)
        + contract_cols(d_outgate_b, w_outgate)
        + contract_cols(d_beta_b, w_beta)
        + contract_cols(d_decay_b, w_decay)
    )
    d_input_norm, grad_attn_gain = norm_pull(d_normed)
    input_grad = (d_resid + d_input_norm).astype(jnp.bfloat16)
    trunk_widths = [
        1,
        w_query.shape[1],
        w_key.shape[1],
        w_value.shape[1],
        w_outgate.shape[1],
        w_beta.shape[1],
        w_decay.shape[1],
    ]
    gain_column = grad_mlp_gain[:, None]
    trunk_gain_column = grad_attn_gain[:, None]
    every_sum = split_columns(
        lax.psum_scatter(
            jnp.concatenate(
                [
                    jnp.concatenate(
                        [
                            trunk_gain_column,
                            contract_rows(normed_b, d_query_b),
                            contract_rows(normed_b, key_block_cotangent),
                            contract_rows(normed_b, d_value_b),
                            contract_rows(normed_b, d_outgate_b),
                            contract_rows(normed_b, d_beta_b),
                            contract_rows(normed_b, d_decay_b),
                        ],
                        axis=1,
                    ),
                    jnp.concatenate(
                        [
                            contract_rows(d_branch_b, gated_b),
                            contract_rows(mlp_b, d_gate_b),
                            contract_rows(mlp_b, d_up_b),
                            contract_rows(out_grad, hidden_b),
                            gain_column,
                        ],
                        axis=1,
                    ),
                ],
                axis=1,
            ),
            ("dp", "seq"),
            scatter_dimension=0,
            tiled=True,
        ),
        trunk_widths + branch_widths,
    )
    trunk_sums = every_sum[:7]
    branch_sums = every_sum[7:]
    small_sums = lax.psum(
        (
            grad_conv_query,
            grad_conv_key,
            grad_conv_value,
            grad_out_gain,
            grad_beta_bias,
            grad_decay_rate,
        ),
        ("dp", "seq"),
    )
    return (
        block_output,
        input_grad,
        trunk_sums[0][:, 0],
        trunk_sums[1],
        trunk_sums[2],
        trunk_sums[3],
        trunk_sums[4],
        trunk_sums[5],
        trunk_sums[6],
        small_sums[4],
        small_sums[5],
        small_sums[0],
        small_sums[1],
        small_sums[2],
        small_sums[3],
        branch_sums[0].T,
        branch_sums[4][:, 0],
        branch_sums[1],
        branch_sums[2],
        branch_sums[3].T,
    )


def solution(mesh):
    in_specs = (
        P(("dp", "seq"), None),
        P("dp", None),
        P(),
        P(),
        P(),
        P(),
        P(),
        P(),
        P(),
        P(),
        P(),
        P(),
        P(),
        P(),
        P(),
        P(),
        P(),
        P(),
        P(),
        P(),
        P(("dp", "seq"), None),
    )
    out_specs = (
        P(("dp", "seq"), None),
        P(("dp", "seq"), None),
        P(("dp", "seq")),
        P(("dp", "seq"), None),
        P(("dp", "seq"), None),
        P(("dp", "seq"), None),
        P(("dp", "seq"), None),
        P(("dp", "seq"), None),
        P(("dp", "seq"), None),
        P(),
        P(),
        P(),
        P(),
        P(),
        P(),
        P(None, ("dp", "seq")),
        P(("dp", "seq")),
        P(("dp", "seq"), None),
        P(("dp", "seq"), None),
        P(None, ("dp", "seq")),
    )
    return jax.shard_map(
        per_device, mesh=mesh, in_specs=in_specs, out_specs=out_specs, check_vma=False
    )
```

profile of v0, /device:TPU:0, one launch (start us, length us, event | category | flops | bytes accessed | tf_op | source)
XLA Modules:
  0.0 1878.8 jit_solution(7467498464250934126)
XLA Ops:
  13.7 5.0 collective-permute-start.1
  64.1 316.0 %custom-call.10 = f32[4,8,1,128,128]{3,4,2,1,0:T(8,128)} custom-call(f32[4,8,1,128,128]{4,3,2,1,0:T(8,128)} %get-tuple-element.799), custom_call_target="InvertDiagBlocksLowerTriangular" | custom-call | tf_op jit(solution)/shard_map/jvp(jit(_solve_triangular))/vmap(vmap())/triangular_solve | solution.py:180
  380.1 6.6 fusion.37
  386.7 5.5 fusion.45
  392.2 5.8 multiply_subtract_fusion
  402.0 28.9 %while.65 = (s32[]{:T(128)}, f32[8,128,128]{2,1,0:T(8,128)}, f32[8,128,128]{2,1,0:T(8,128)}, f32[4,8,128,128]{3,2,1,0:T(8,128)}, f32[4,8,128,128]{3,2,1,0:T(8,12...) while((s32[]{:T(128)}, f32[8,128,128]{2,1,0:T(8,128)}, ...), condition=%wide.region_7.8_spmd.clone, body=%wide.region_6.7_spmd.clone.sunk | while | flops 403046400 | bytes 16254611 | solution.py:204
  452.3 5.4 slice.193
  469.4 39.7 %all-gather.11.cloned.1.call-done = bf16[128,128,128]{2,1,0:T(8,128)(2,1)} async-done(((bf16[8,128,128]{2,1,0:T(8,128)(2,1)}), bf16[128,128,128]{2,1,0:T(8,128)(2,1)}) %all-gather.11.cloned.1.call-update) | async-done | bytes 4194320 | tf_op jit(solution)/shard_map/all_gather | solution.py:27
  509.1 78.1 %all-gather.9.cloned.1.call-done = bf16[128,128,128]{2,1,0:T(8,128)(2,1)} async-done(((bf16[8,128,128]{2,1,0:T(8,128)(2,1)}), bf16[128,128,128]{2,1,0:T(8,128)(2,1)}) %all-gather.9.cloned.1.call-update) | async-done | bytes 4194320 | tf_op jit(solution)/shard_map/all_gather | solution.py:27
  590.9 4.6 multiply_reduce_fusion.23
  607.0 9.3 multiply_convert_fusion
  630.9 4.7 mul.1037.clone
  635.7 4.4 mul.1141
  642.1 4.2 fusion.155
  646.3 4.3 fusion.118
  650.6 4.2 fusion.67
  654.8 5.3 fusion.241
  673.9 4.8 fusion.153
  678.7 4.8 fusion.249
  683.5 4.8 fusion.250
  694.0 6.2 fusion.252
  700.2 5.9 fusion.251
  706.1 6.1 convolution_bitcast_fusion
  712.2 4.8 fusion.157
  718.4 20.0 %pad.107 = f32[4,8,128]{1,0,2:T(4,128)} pad(f32[4,8,64]{1,0,2:T(4,128)S(1)} %copy.458, f32[]{:T(128)} %constant.174.clone.1), padding=0_0_0x0_0_0x1_0_1 | pad | bytes 24580 | tf_op jit(solution)/shard_map/transpose(jvp())/pad | solution.py:187
  738.3 16.7 pad.108
  758.6 8.3 rev.6
  766.9 48.2 %all-gather.15.cloned.1.call-done = f32[128,128,128]{2,1,0:T(8,128)} async-done(((f32[8,128,128]{2,1,0:T(8,128)}), f32[128,128,128]{2,1,0:T(8,128)}) %all-gather.15.cloned.1.call-update) | async-done | bytes 8388624 | tf_op jit(solution)/shard_map/all_gather | solution.py:46
  815.1 7.8 rev.7
  822.9 56.2 %while.66 = (s32[]{:T(128)}, f32[8,128,128]{2,1,0:T(8,128)}, s32[]{:T(128)}, f32[16,8,128,128]{3,2,1,0:T(8,128)}, f32[16,8,128,128]{3,2,1,0:T(8,128)}, /*index=5*/s32[]{:T(128)}, s32[]{:T(128)}) while((s32[]{:T(128)}, f32[8,128,128]{2,1,0:T(8,128)}, s32[]{:T(128)}, f32[16,8,128,128]{3,2,1,0:T(8,128)}, ...), condition=%wide.region_16.17_spmd.clone, body=%wide.region_15.16_spmd.clone.sunk | while | flops 201850880 | bytes 3672679 | solution.py:57
  885.3 56.1 %while.64 = (s32[]{:T(128)}, f32[8,128,128]{2,1,0:T(8,128)}, f32[8,128,128]{2,1,0:T(8,128)}, f32[4,8,128,128]{2,3,1,0:T(8,128)}, f32[4,8,128,128]{3,2,1,0:T(8,12...) while((s32[]{:T(128)}, f32[8,128,128]{2,1,0:T(8,128)}, ...), condition=%wide.region_18.19_spmd, body=%wide.region_17.18_spmd.sunk | while | flops 805699584 | bytes 11013257 | solution.py:204
  941.4 4.8 fusion.87
  946.3 4.5 fusion.84
  950.8 4.8 fusion.41
  955.6 5.3 fusion.42
  960.9 4.5 fusion.57
  969.1 4.5 fusion.90
  975.4 5.4 fusion.64
  983.4 11.3 multiply_reduce_fusion.10
  994.8 5.0 add_add_fusion.1
  1011.0 5.0 reduce_window_sum.30
  1032.1 10.8 multiply_reduce_fusion.7
  1052.9 4.7 fusion.163
  1061.1 4.6 fusion.161
  1070.7 74.5 %concatenate.38 = f32[1024,15642]{1,0:T(8,128)} concatenate(f32[1024,1]{1,0:T(8,128)S(1)} %copy.467, f32[1024,1024]{1,0:T(8,128)} %fusion.174, f32[1024,2048]{1,0:T(8,128)} %fusion.163, f32[1024,2048]{1,0:T(8,128)} %fusion.161, f32[1024,1024]{1,0:T(8,128)} %fusion.215, f32[1024,16]{1,0:T(8,128)S(1)} %fusion.213, f32[1024,8]{1,0:T(8,128)S(1)} %fusion.211, f32[1024,1024]{1,0:T(8,128)} %fusion.175, ...), dimensions={1} | concatenate | bytes 128139264 | tf_op jit(solution)/shard_map/concatenate | solution.py:402
  1146.5 5.5 fusion.109
  1157.1 576.6 %reduce-scatter.2.cloned.1.call-done = f32[32,15642]{1,0:T(8,128)} async-done(((f32[1024,15642]{1,0:T(8,128)}), f32[32,15642]{1,0:T(8,128)}) %reduce-scatter.2.cloned.1.call-update) | async-done | bytes 2002192 | tf_op jit(solution)/shard_map/reduce_scatter | solution.py:401
  1744.4 119.8 %all-reduce.34.cloned.1.call-done = (f32[16]{0:T(128)}, f32[8]{0:T(128)}, f32[4,1024]{1,0:T(4,128)}, f32[4,2048]{1,0:T(4,128)}, f32[4,2048]{1,0:T(4,128)}, /*index=5*/f32[128]{0:T(128)}) async-done(((f32[16]{0:T(128)}, f32[8]{0:T(128)}, f32[4,1024]{1,0:T(4,128)}, f32[4,2048]{1,0:T(4,128)}, f32[4,2048]{1,0:T(4,128)}, /*index=5*/f32[128]{0:T(128)}), (f32[16]{0:T(128)}, f32[8]{0:T(128)}, f32[4,1024]{1,0:T(4,128)}, ...) | async-done | bytes 82544 | tf_op jit(solution)/shard_map/psum | solution.py:437
  (653 shorter events, 369.1 us)
Async XLA Ops:
  7.2 592.3 %copy-start = (bf16[1024,1024]{1,0:T(8,128)(2,1)S(1)}, bf16[1024,1024]{1,0:T(8,128)(2,1)}, u32[]{:S(2)}) copy-start(bf16[1024,1024]{1,0:T(8,128)(2,1)} %param.44) | copy-start | bytes 6291460
  7.2 501.9 %all-gather.11.cloned.1.call-start = ((), (), s32[]{:S(2)}) async-start(), calls=%async_computation.3 | async-start | bytes 4456448 | tf_op jit(solution)/shard_map/all_gather | solution.py:27
  13.7 10.1 copy-start.163
  13.7 11.0 copy-start.142
  13.7 26.9 %collective-permute-start.1 = (bf16[3,2048]{1,0:T(4,128)(2,1)}, bf16[3,2048]{1,0:T(4,128)(2,1)S(1)}, u32[]{:S(2)}, u32[]{:S(2)}) collective-permute-start(bf16[3,2048]{1,0:T(4,128)(2,1)} %slice.251), channel_id=1, source_target_pairs={{0,1},{1,2},{2,3},{3,4},{4,5},{5,6},{6,7},{7,8},{8,9},{9,10},{10,1... | collective-permute-start | bytes 36872 | tf_op jit(solution)/shard_map/ppermute | solution.py:21
  20.2 10.2 collective-permute-start.2
  23.8 36.0 %copy-start.99 = (pred[128,128]{1,0:T(8,128)(4,1)}, pred[128,128]{1,0:T(8,128)(4,1)S(1)}, u32[]{:S(2)}) copy-start(pred[128,128]{1,0:T(8,128)(4,1)S(1)} %get-tuple-element.850) | copy-start | bytes 49156
  23.8 374.2 %copy-start.84 = (f32[128,128]{1,0:T(8,128)}, f32[128,128]{1,0:T(8,128)S(1)}, u32[]{:S(2)}) copy-start(f32[128,128]{1,0:T(8,128)S(1)} %get-tuple-element.851) | copy-start | bytes 196612
  24.7 645.2 %copy-start.132 = (f32[256]{0:T(256)}, f32[256]{0:T(256)S(1)}, u32[]{:S(2)}) copy-start(f32[256]{0:T(256)S(1)} %get-tuple-element.824) | copy-start | bytes 3076
  24.7 645.2 %copy-start.134 = (f32[256]{0:T(256)}, f32[256]{0:T(256)S(1)}, u32[]{:S(2)}) copy-start(f32[256]{0:T(256)S(1)} %get-tuple-element.825) | copy-start | bytes 3076
  27.1 32.6 %copy-start.94 = (f32[4,8,128]{2,1,0:T(8,128)}, f32[4,8,128]{2,1,0:T(8,128)S(1)}, u32[]{:S(2)}) copy-start(f32[4,8,128]{2,1,0:T(8,128)S(1)} %reduce_window_sum.29) | copy-start | bytes 49156
  28.0 31.7 %copy-start.105 = (pred[128,128]{1,0:T(8,128)(4,1)}, pred[128,128]{1,0:T(8,128)(4,1)S(1)}, u32[]{:S(2)}) copy-start(pred[128,128]{1,0:T(8,128)(4,1)S(1)} %get-tuple-element.848) | copy-start | bytes 49156
  28.0 31.7 %copy-start.108 = (pred[128,128]{1,0:T(8,128)(4,1)}, pred[128,128]{1,0:T(8,128)(4,1)S(1)}, u32[]{:S(2)}) copy-start(pred[128,128]{1,0:T(8,128)(4,1)S(1)} %get-tuple-element.849) | copy-start | bytes 49156
  28.5 12.5 copy-start.113
  28.5 12.5 copy-start.115
  28.6 12.5 copy-start.117
  28.6 12.5 copy-start.119
  30.3 29.5 %copy-start.103 = (f32[4,8,128]{2,1,0:T(8,128)}, f32[4,8,128]{2,1,0:T(8,128)S(1)}, u32[]{:S(2)}) copy-start(f32[4,8,128]{2,1,0:T(8,128)S(1)} %copy.406) | copy-start | bytes 49156
  30.4 27.4 %copy-start.101 = (f32[4,8,128]{2,1,0:T(8,128)}, f32[4,8,128]{2,1,0:T(8,128)S(1)}, u32[]{:S(2)}) copy-start(f32[4,8,128]{2,1,0:T(8,128)S(1)} %copy.411) | copy-start | bytes 49156
  386.7 13.7 copy-start.5
  432.7 154.4 %all-gather.9.cloned.1.call-start = ((), (), s32[]{:S(2)}) async-start(), calls=%async_computation.2 | async-start | bytes 4456448 | tf_op jit(solution)/shard_map/all_gather | solution.py:27
  434.6 324.0 %all-gather.13.cloned.1.call-start = ((), (), s32[]{:S(2)}) async-start(), calls=%async_computation.4 | async-start | bytes 8912896 | tf_op jit(solution)/shard_map/all_gather | solution.py:46
  436.7 378.4 %all-gather.15.cloned.1.call-start = ((), (), s32[]{:S(2)}) async-start(), calls=%async_computation.5 | async-start | bytes 8912896 | tf_op jit(solution)/shard_map/all_gather | solution.py:46
  439.4 5.2 collective-permute-start
  600.3 19.6 %copy-start.48 = (f32[256,1024]{1,0:T(8,128)}, f32[256,1024]{1,0:T(8,128)S(1)}, u32[]{:S(2)}) copy-start(f32[256,1024]{1,0:T(8,128)S(1)} %get-tuple-element.836) | copy-start | bytes 3145732
  628.5 1105.1 %reduce-scatter.2.cloned.1.call-start = ((), (), s32[]{:S(2)}) async-start(), calls=%async_computation.1 | async-start | bytes 66502656 | tf_op jit(solution)/shard_map/reduce_scatter | solution.py:401
  672.5 82.5 %collective-permute-start.3 = (bf16[3,1024]{1,0:T(4,128)(2,1)S(1)}, bf16[3,1024]{1,0:T(4,128)(2,1)S(1)}, u32[]{:S(2)}, u32[]{:S(2)}) collective-permute-start(bf16[3,1024]{1,0:T(4,128)(2,1)S(1)} %slice.266), channel_id=1, source_target_pairs={{1,0},{2,1},{3,2},{4,3},{5,4},{6,5},{7,6},{8,7},{9,8},{10,9},{11,1... | collective-permute-start | bytes 18440 | tf_op jit(solution)/shard_map/ppermute | solution.py:21
  717.2 38.6 %copy-start.61 = (bf16[253,1024]{1,0:T(8,128)(2,1)}, bf16[253,1024]{1,0:T(8,128)(2,1)S(1)}, u32[]{:S(2)}) copy-start(bf16[253,1024]{1,0:T(8,128)(2,1)S(1)} %slice.264) | copy-start | bytes 1554436
  969.1 11.7 copy-start.85
  969.1 13.7 copy-start.69
  983.4 11.3 copy-start.35
  983.4 11.3 copy-start.40
  983.4 11.3 copy-start.45
  983.4 11.3 copy-start.47
  983.4 11.3 copy-start.72
  983.4 11.3 copy-start.102
  1032.0 10.9 copy-start.114
  1032.0 10.9 copy-start.116
  1032.1 10.9 copy-start.118
  1032.1 10.9 copy-start.120
  1032.1 10.9 copy-start.122
  1032.1 10.9 copy-start.124
  1032.1 10.9 copy-start.126
  1032.1 10.8 copy-start.128
  1047.2 5.6 collective-permute-start.4
  1050.7 8.2 collective-permute-start.5
  1145.2 719.0 %all-reduce.34.cloned.1.call-start = ((), (), s32[]{:S(2)}) async-start(), calls=%async_computation.6 | async-start | bytes 166912 | tf_op jit(solution)/shard_map/psum | solution.py:437
  1153.9 717.9 %copy-start.1 = (bf16[1024,1024]{1,0:T(8,128)(2,1)S(1)}, bf16[1024,1024]{1,0:T(8,128)(2,1)}, u32[]{:S(2)}) copy-start(bf16[1024,1024]{1,0:T(8,128)(2,1)} %param.44) | copy-start | bytes 6291460
  (136 other events, 511.1 us)
Sparse Core Ops, SparseCore 0:
  432.8 76.2 all-gather.10
  512.4 74.6 all-gather.8
  589.9 111.4 all-gather.12
  704.0 111.0 all-gather.14
  1145.3 588.2 reduce-scatter.1
  1741.6 122.5 all-reduce.33
where the time goes:
time: 1890 us; the launch traced here: 1880 us
  waiting for transfers between devices  863 us (46%)
  other arithmetic  398 us (21%)
  matrix products  317 us (17%)
  local copies, waits for them, and re-layouts  267 us (14%)
    reduce_scatter x1, waiting for transfers between devices, per_device(): lax.psum_scatter(jnp.concatenate([jnp.concatenate([trunk_gain_column, con...  577 us
    another operation x4, other arithmetic, mixer_local(): jax.scipy.linalg.solve_triangular(system, rhs, lower=True, unit_diagonal=...  319 us
    psum x1, waiting for transfers between devices, per_device(): lax.psum((grad_conv_query, grad_conv_key, grad_conv_value, grad_out_gain,...  120 us
    all_gather x2, waiting for transfers between devices, prefix_2(): lax.all_gather(a.astype(kind), axis)  118 us
    concatenate x1, local copies, waits for them, and re-layouts, per_device(): jnp.concatenate([jnp.concatenate([trunk_gain_column, contract_rows(normed...  74.5 us
    dot_general x27, matrix products, compose_maps(): jnp.einsum('hij,hjk->hik', later[0], earlier[1], precision=EXACT_PRECISION)  71.1 us
    all_gather x2, waiting for transfers between devices, prefix_3(): pieces = jax.tree.map(lambda part: lax.all_gather(part, axis), value)  48.2 us
  transfers between devices with their start and end apart: 12, of which 6 were waited for; matrix products, arithmetic and copies ran while one was open for 13% of the time, Pallas kernels for 0%

commit v1 on v0

v1 whole, which is shorter than its diff:
```python
from functools import partial

import jax
import jax.numpy as jnp
from jax import lax
from jax.experimental import pallas as pl
from jax.experimental.pallas import tpu as pltpu
from jax.sharding import PartitionSpec as P

REFLECTS = 2
KW = 4
BLOCK = 64
SHORTEST = 1024
STEPS = BLOCK * REFLECTS
HALO = 8
RESET_LOG = -80.0
MESH = pl.DeviceIdType.MESH
F32 = jnp.float32
BF16 = jnp.bfloat16
NN = (((1,), (0,)), ((), ()))
NT = (((1,), (1,)), ((), ()))
TN = (((0,), (0,)), ((), ()))
VMEM_LIMIT = 56 * 1024 * 1024


def mm(a, b, dims=NN):
    return lax.dot_general(a.astype(BF16), b.astype(BF16), dims, preferred_element_type=F32)


def halves(a):
    high = a.astype(BF16)
    return high, (a - high.astype(F32)).astype(BF16)


def mm3(a, b):
    ah, al = halves(a)
    bh, bl = halves(b)
    return mm(ah, bh) + (mm(ah, bl) + mm(al, bh))


def mm2(a, b, dims=NN):
    ah, al = halves(a)
    return mm(ah, b, dims) + mm(al, b, dims)


def sigmoid(v):
    return 1.0 / (1.0 + jnp.exp(-v))


def step_ids(shape, axis):
    index = lax.broadcasted_iota(jnp.int32, shape, axis)
    return index % BLOCK, index // BLOCK


def step_masks():
    shape = (STEPS, STEPS)
    tm, jm = step_ids(shape, 0)
    tn, jn = step_ids(shape, 1)
    strict = (tm > tn) | ((tm == tn) & (jm > jn))
    size = 4
    first = tm // size == tn // size
    merges = []
    while size < BLOCK:
        merges.append((tm // (2 * size) == tn // (2 * size)) & (tm // size != tn // size))
        size = 2 * size
    eye = ((tm == tn) & (jm == jn)).astype(F32)
    return tm >= tn, strict, first, merges, eye


def unit_lower_inverse(systems, first, merges, eye):
    neg = [jnp.where(first, -a, 0.0) for a in systems]
    inv = [eye + n for n in neg]
    for _ in range(2):
        neg = [mm3(n, n) for n in neg]
        inv = [t + mm3(t, n) for t, n in zip(inv, neg)]
    for merge in merges:
        off = [mm3(jnp.where(merge, a, 0.0), t) for a, t in zip(systems, inv)]
        inv = [t - mm3(t, o) for t, o in zip(inv, off)]
    return inv


def conv_parts(ext_ref, taps, live, columns, rows):
    total = None
    for back in range(KW):
        part = ext_ref[pl.ds(HALO - back, rows), columns] * taps[KW - 1 - back : KW - back, :]
        if back > 0:
            part = part * live[:, back : back + 1]
        total = part if total is None else total + part
    return total


def head_features(ext_ref, tq, tk, tv, live, rows, width):
    conv = [
        conv_parts(ext_ref, tq[...], live, pl.ds(0, width), rows),
        conv_parts(ext_ref, tk[:, :width], live, pl.ds(width, width), rows),
        conv_parts(ext_ref, tk[:, width:], live, pl.ds(2 * width, width), rows),
        conv_parts(ext_ref, tv[:, :width], live, pl.ds(3 * width, width), rows),
        conv_parts(ext_ref, tv[:, width:], live, pl.ds(4 * width, width), rows),
    ]
    return conv


def unit_rows(act):
    return lax.rsqrt(jnp.sum(act * act, axis=-1, keepdims=True) + 1e-06)


def mixer_forward_kernel(
    xn_ref, wq_ref, wk_ref, wv_ref, wg_ref, tq_ref, tk_ref, tv_ref, live_ref, acol_ref, arow_ref,
    pre_ref, gate_ref, oloc_ref, oread_ref, inv_ref, delta_ref, state_ref, final_ref,
    ext_ref,
):
    rows, width = oloc_ref.shape
    blocks = rows // BLOCK
    xn = xn_ref[...]
    pre = jnp.concatenate(
        [mm(xn, wq_ref[...]), mm(xn, wk_ref[...]), mm(xn, wv_ref[...])], axis=1
    ).astype(BF16)
    pre_ref[0] = pre
    ext_ref[...] = pre.astype(F32)
    gate_ref[...] = mm(xn[HALO:], wg_ref[...])
    live = live_ref[...]
    conv = head_features(ext_ref, tq_ref, tk_ref, tv_ref, live, rows, width)
    act = [c * sigmoid(c) for c in conv]
    q = (act[0] * unit_rows(act[0]) * width ** (-0.5)).astype(BF16)
    k = [(a * unit_rows(a)).astype(BF16) for a in act[1:3]]
    v = [a.astype(BF16) for a in act[3:5]]
    reach, strict, first, merges, eye = step_masks()
    cut = [slice(b * BLOCK, (b + 1) * BLOCK) for b in range(blocks)]
    kb = [jnp.concatenate([k[0][s], k[1][s]], axis=0) for s in cut]
    vb = [jnp.concatenate([v[0][s], v[1][s]], axis=0) for s in cut]
    qb = [q[s] for s in cut]
    ccol = [acol_ref[0, b, :, 0:1] for b in range(blocks)]
    bcol = [acol_ref[0, b, :, 1:2] for b in range(blocks)]
    crow = [arow_ref[0, b, 0:1, :] for b in range(blocks)]
    brow = [arow_ref[0, b, 1:2, :] for b in range(blocks)]
    fade = [jnp.exp(jnp.where(reach, c - r, -1e30)) for c, r in zip(ccol, crow)]
    gram = [mm(x, x, NT) for x in kb]
    system = [jnp.where(strict, f * g, 0.0) * b for f, g, b in zip(fade, gram, bcol)]
    inv = unit_lower_inverse(system, first, merges, eye)
    for b in range(blocks):
        inv_ref[0, b] = inv[b]
    local = [mm2(t * b, x) for t, b, x in zip(inv, brow, vb)]
    reads = [mm2(t * (b * jnp.exp(c)), x) for t, b, c, x in zip(inv, brow, crow, kb)]
    score = [f[:BLOCK] * mm(x, y, NT) for f, x, y in zip(fade, qb, kb)]
    state = jnp.concatenate([jnp.zeros((width, width), F32), eye], axis=1)
    for b in range(blocks):
        state_ref[0, b] = state
        grow = jnp.exp(ccol[b])
        last = ccol[b][BLOCK - 1 : BLOCK]
        if b == 0:
            delta = jnp.concatenate([local[b], -reads[b]], axis=1)
        else:
            delta = jnp.concatenate([local[b], jnp.zeros((STEPS, width), F32)], axis=1) - mm(
                reads[b], state
            )
        delta_ref[0, b] = delta
        out = mm(score[b], delta) + grow[:BLOCK] * mm(qb[b], state)
        oloc_ref[cut[b], :] = out[:, :width]
        oread_ref[0, cut[b], :] = out[:, width:]
        tail = kb[b].astype(F32) * jnp.exp(last - ccol[b])
        state = jnp.exp(last) * state + mm(tail, delta, TN)
    final_ref[0] = state.astype(BF16)


def head_columns(rows, width):
    return pl.BlockSpec((rows, width), lambda h: (0, h))


def whole(shape):
    return pl.BlockSpec(shape, lambda h: (0,) * len(shape))


def per_head(shape):
    return pl.BlockSpec((1,) + shape, lambda h: (h,) + (0,) * len(shape))


def mixer_forward(xn, w_query, w_key, w_value, w_outgate, taps, live, acol, arow, heads, width):
    ext_rows, depth = xn.shape
    rows = ext_rows - HALO
    blocks = rows // BLOCK
    conv_query, conv_key, conv_value = taps
    out = jax.ShapeDtypeStruct
    return pl.pallas_call(
        mixer_forward_kernel,
        grid=(heads,),
        in_specs=[
            whole((ext_rows, depth)),
            head_columns(depth, width),
            head_columns(depth, 2 * width),
            head_columns(depth, 2 * width),
            head_columns(depth, width),
            head_columns(KW, width),
            head_columns(KW, 2 * width),
            head_columns(KW, 2 * width),
            whole(live.shape),
            per_head(acol.shape[1:]),
            per_head(arow.shape[1:]),
        ],
        out_specs=[
            per_head((ext_rows, 5 * width)),
            head_columns(rows, width),
            head_columns(rows, width),
            per_head((rows, width)),
            per_head((blocks, STEPS, STEPS)),
            per_head((blocks, STEPS, 2 * width)),
            per_head((blocks, width, 2 * width)),
            per_head((width, 2 * width)),
        ],
        out_shape=[
            out((heads, ext_rows, 5 * width), BF16),
            out((rows, heads * width), F32),
            out((rows, heads * width), F32),
            out((heads, rows, width), F32),
            out((heads, blocks, STEPS, STEPS), F32),
            out((heads, blocks, STEPS, 2 * width), F32),
            out((heads, blocks, width, 2 * width), F32),
            out((heads, width, 2 * width), BF16),
        ],
        scratch_shapes=[pltpu.VMEM((ext_rows, 5 * width), F32)],
        compiler_params=pltpu.CompilerParams(vmem_limit_bytes=VMEM_LIMIT),
        name="mixer_forward",
    )(xn, w_query, w_key, w_value, w_outgate, conv_query, conv_key, conv_value, live, acol, arow)


def conv_pull(ext_ref, pad_ref, d_conv, taps, live, columns, rows, dtap_ref):
    total = None
    for back in range(KW):
        part = d_conv if back == 0 else d_conv * live[:, back : back + 1]
        source = ext_ref[pl.ds(HALO - back, rows), columns]
        dtap_ref[KW - 1 - back : KW - back, :] = jnp.sum(part * source, axis=0, keepdims=True)
        pad_ref[pl.ds(HALO, rows), :] = part
        moved = pad_ref[pl.ds(back, rows + HALO), :] * taps[KW - 1 - back : KW - back, :]
        total = moved if total is None else total + moved
    return total


def silu_pull(c, grad):
    s = sigmoid(c)
    return grad * (s + c * s * (1.0 - s))


def unit_pull(act, grad, scale):
    r = unit_rows(act)
    return scale * r * (grad - act * (r * r * jnp.sum(act * grad, axis=-1, keepdims=True)))


def mixer_backward_kernel(
    pre_ref, tq_ref, tk_ref, tv_ref, live_ref, acol_ref, arow_ref,
    inv_ref, delta_ref, state_ref, start_ref, after_ref, dout_ref,
    dq_ref, dk_ref, dv_ref, rimq_ref, rimk_ref, rimv_ref, dtq_ref, dtk_ref, dtv_ref, aux_ref,
    ext_ref, pad_ref,
):
    rows, width = dout_ref.shape
    blocks = rows // BLOCK
    ext_ref[...] = pre_ref[0].astype(F32)
    live = live_ref[...]
    conv = head_features(ext_ref, tq_ref, tk_ref, tv_ref, live, rows, width)
    act = [c * sigmoid(c) for c in conv]
    q = (act[0] * unit_rows(act[0]) * width ** (-0.5)).astype(BF16)
    k = [(a * unit_rows(a)).astype(BF16) for a in act[1:3]]
    reach, strict, _, _, _ = step_masks()
    start = start_ref[0]
    after = after_ref[0].astype(F32)
    pieces = [None] * blocks
    for b in range(blocks - 1, -1, -1):
        s = slice(b * BLOCK, (b + 1) * BLOCK)
        kb = jnp.concatenate([k[0][s], k[1][s]], axis=0)
        kf = kb.astype(F32)
        qb = q[s]
        ccol = acol_ref[0, b, :, 0:1]
        bcol = acol_ref[0, b, :, 1:2]
        crow = arow_ref[0, b, 0:1, :]
        last = ccol[BLOCK - 1 : BLOCK]
        fade = jnp.exp(jnp.where(reach, ccol - crow, -1e30))
        grow = jnp.exp(ccol)
        weight = jnp.exp(last - ccol)
        dout = dout_ref[s, :]
        gdout = grow[:BLOCK] * dout
        delta = delta_ref[0, b, :, :width] + mm(delta_ref[0, b, :, width:], start)
        state = state_ref[0, b, :, :width] + mm(state_ref[0, b, :, width:], start)
        fade_q = fade[:BLOCK]
        score = fade_q * mm(qb, kb, NT)
        d_delta = mm(score, dout, TN) + weight * mm(kb, after)
        d_rhs = mm(inv_ref[0, b], d_delta, TN)
        d_score = fade_q * mm(dout, delta, NT)
        d_known = -(bcol * grow) * d_rhs
        d_tail = weight * mm(delta, after, NT)
        d_gram = jnp.where(strict, -bcol * fade * mm(d_rhs, delta, NT), 0.0)
        dq = mm(gdout, state, NT) + mm(d_score, kb)
        dk_row = mm(d_known, state, NT) + mm(d_gram, kb)
        dk_col = mm(d_gram, kb, TN) + mm(d_score, qb, TN) + d_tail
        d_beta = (1.0 - bcol) * jnp.sum(d_rhs * delta, axis=-1, keepdims=True)
        d_log = jnp.sum(kf * (dk_row - dk_col), axis=-1, keepdims=True)
        d_logq = jnp.sum(qb.astype(F32) * dq, axis=-1, keepdims=True)
        d_last = jnp.sum(kf * d_tail) + jnp.sum(jnp.exp(last) * after * state)
        tok = lax.broadcasted_iota(jnp.int32, (BLOCK, 1), 0)
        d_token = d_log[:BLOCK] + d_log[BLOCK:] + d_logq
        d_token = d_token + jnp.where(tok == BLOCK - 1, d_last, 0.0)
        aux_ref[0, b, :, 0:1] = d_beta
        aux_ref[0, b, 0:BLOCK, 1:2] = d_token
        dk = dk_row + dk_col
        pieces[b] = (dq, dk[:BLOCK], dk[BLOCK:], (bcol * d_rhs)[:BLOCK], (bcol * d_rhs)[BLOCK:])
        after = jnp.exp(last) * after + mm(qb, gdout, TN) + mm(kb, d_known, TN)
    d_act = [jnp.concatenate([pieces[b][i] for b in range(blocks)], axis=0) for i in range(5)]
    d_act[0] = unit_pull(act[0], d_act[0], width ** (-0.5))
    d_act[1] = unit_pull(act[1], d_act[1], 1.0)
    d_act[2] = unit_pull(act[2], d_act[2], 1.0)
    d_conv = [silu_pull(c, g) for c, g in zip(conv, d_act)]
    pad_ref[0:HALO, :] = jnp.zeros((HALO, width), F32)
    pad_ref[pl.ds(HALO + rows, HALO), :] = jnp.zeros((HALO, width), F32)
    sides = (
        (tq_ref, dq_ref, rimq_ref, dtq_ref, 0),
        (tk_ref, dk_ref, rimk_ref, dtk_ref, 0),
        (tk_ref, dk_ref, rimk_ref, dtk_ref, width),
        (tv_ref, dv_ref, rimv_ref, dtv_ref, 0),
        (tv_ref, dv_ref, rimv_ref, dtv_ref, width),
    )
    for i, (tap_ref, d_ref, rim_ref, dtap_ref, at) in enumerate(sides):
        lanes = pl.ds(at, width)
        grad = conv_pull(
            ext_ref, pad_ref, d_conv[i], tap_ref[:, lanes], live, pl.ds(i * width, width), rows,
            dtap_ref.at[:, lanes],
        )
        rim_ref[:, lanes] = grad[:HALO].astype(BF16)
        d_ref[:, lanes] = grad[HALO:].astype(BF16)


def mixer_backward(pre, taps, live, acol, arow, inv, delta, state, start, after, dout):
    heads, ext_rows, _ = pre.shape
    rows = ext_rows - HALO
    width = start.shape[-1]
    conv_query, conv_key, conv_value = taps
    out = jax.ShapeDtypeStruct
    columns = heads * width
    return pl.pallas_call(
        mixer_backward_kernel,
        grid=(heads,),
        in_specs=[
            per_head(pre.shape[1:]),
            head_columns(KW, width),
            head_columns(KW, 2 * width),
            head_columns(KW, 2 * width),
            whole(live.shape),
            per_head(acol.shape[1:]),
            per_head(arow.shape[1:]),
            per_head(inv.shape[1:]),
            per_head(delta.shape[1:]),
            per_head(state.shape[1:]),
            per_head((width, width)),
            per_head((width, width)),
            head_columns(rows, width),
        ],
        out_specs=[
            head_columns(rows, width),
            head_columns(rows, 2 * width),
            head_columns(rows, 2 * width),
            head_columns(HALO, width),
            head_columns(HALO, 2 * width),
            head_columns(HALO, 2 * width),
            head_columns(KW, width),
            head_columns(KW, 2 * width),
            head_columns(KW, 2 * width),
            per_head(acol.shape[1:]),
        ],
        out_shape=[
            out((rows, columns), BF16),
            out((rows, 2 * columns), BF16),
            out((rows, 2 * columns), BF16),
            out((HALO, columns), BF16),
            out((HALO, 2 * columns), BF16),
            out((HALO, 2 * columns), BF16),
            out((KW, columns), F32),
            out((KW, 2 * columns), F32),
            out((KW, 2 * columns), F32),
            out(acol.shape, F32),
        ],
        scratch_shapes=[
            pltpu.VMEM((ext_rows, 5 * width), F32),
            pltpu.VMEM((rows + 2 * HALO, width), F32),
        ],
        compiler_params=pltpu.CompilerParams(vmem_limit_bytes=VMEM_LIMIT),
        name="mixer_backward",
    )(pre, conv_query, conv_key, conv_value, live, acol, arow, inv, delta, state, start, after, dout)


def gated_forward_kernel(oloc_ref, oread_ref, start_ref, gate_ref, gain_ref, out_ref, gated_ref):
    out = oloc_ref[...] + mm(oread_ref[0], start_ref[0])
    out_ref[...] = out
    gate = gate_ref[...]
    r = lax.rsqrt(jnp.mean(out * out, axis=-1, keepdims=True) + 1e-05)
    gated_ref[...] = (out * r * gain_ref[...] * (gate * sigmoid(gate))).astype(BF16)


def gated_forward(oloc, oread, start, gate_pre, out_gain):
    heads, rows, width = oread.shape
    out = jax.ShapeDtypeStruct
    return pl.pallas_call(
        gated_forward_kernel,
        grid=(heads,),
        in_specs=[
            head_columns(rows, width),
            per_head((rows, width)),
            per_head((width, width)),
            head_columns(rows, width),
            whole((1, width)),
        ],
        out_specs=[head_columns(rows, width), head_columns(rows, width)],
        out_shape=[out(oloc.shape, F32), out(oloc.shape, BF16)],
        name="gated_forward",
    )(oloc, oread, start, gate_pre, out_gain[None, :])


def gated_backward_kernel(
    out_ref, gate_ref, gain_ref, dgated_ref, oread_ref, dout_ref, dgate_ref, part_ref, dgain_ref
):
    out = out_ref[...]
    gate = gate_ref[...]
    gain = gain_ref[...]
    grad = dgated_ref[...]
    r = lax.rsqrt(jnp.mean(out * out, axis=-1, keepdims=True) + 1e-05)
    s = sigmoid(gate)
    unit = out * r
    dgate_ref[...] = (grad * unit * gain * (s + gate * s * (1.0 - s))).astype(BF16)
    through = grad * (gate * s)
    dgain_ref[0] = jnp.sum(through * unit, axis=0, keepdims=True)
    through = through * gain
    dout = r * (through - unit * jnp.mean(unit * through, axis=-1, keepdims=True))
    dout_ref[...] = dout
    part_ref[0] = mm(oread_ref[0], dout, TN).astype(BF16)


def gated_backward(out_all, gate_pre, out_gain, d_gated, oread):
    heads, rows, width = oread.shape
    out = jax.ShapeDtypeStruct
    return pl.pallas_call(
        gated_backward_kernel,
        grid=(heads,),
        in_specs=[
            head_columns(rows, width),
            head_columns(rows, width),
            whole((1, width)),
            head_columns(rows, width),
            per_head((rows, width)),
        ],
        out_specs=[
            head_columns(rows, width),
            head_columns(rows, width),
            per_head((width, width)),
            per_head((1, width)),
        ],
        out_shape=[
            out(out_all.shape, F32),
            out(out_all.shape, BF16),
            out((heads, width, width), BF16),
            out((heads, 1, width), F32),
        ],
        name="gated_backward",
    )(out_all, gate_pre, out_gain[None, :], d_gated, oread)


def carry_kernel(count, heads, backward, *refs):
    if backward:
        part_ref, maps_ref, result_ref, inbox, outbox, landed, send_sem, recv_sem, back_sem, land_sem = refs
    else:
        part_ref, result_ref, maps_ref, inbox, outbox, landed, send_sem, recv_sem, back_sem, land_sem = refs
    place = lax.axis_index("seq")
    group = lax.axis_index("dp")
    width = result_ref.shape[-1]
    stride = count // 16

    def keeper(h):
        return (2 * h + group) * stride

    barrier = pltpu.get_barrier_semaphore()

    def greet(step, carry):
        peer = lax.rem(place + step, count)
        pl.semaphore_signal(barrier, inc=1, device_id=(group, peer), device_id_type=MESH)
        return carry

    lax.fori_loop(1, count, greet, 0)
    pl.semaphore_wait(barrier, count - 1)

    def outgoing(h):
        return pltpu.make_async_remote_copy(
            src_ref=part_ref.at[h],
            dst_ref=inbox.at[place],
            send_sem=send_sem.at[h],
            recv_sem=recv_sem.at[place],
            device_id=(group, keeper(h)),
            device_id_type=MESH,
        )

    for h in range(heads):

        @pl.when(place != keeper(h))
        def _(h=h):
            outgoing(h).start()

        @pl.when(place == keeper(h))
        def _(h=h):
            inbox[pl.ds(place, 1)] = part_ref[h : h + 1]

    def scan_head(h):
        def returning(where):
            return pltpu.make_async_remote_copy(
                src_ref=outbox.at[where],
                dst_ref=landed.at[h],
                send_sem=back_sem.at[where],
                recv_sem=land_sem.at[h],
                device_id=(group, where),
                device_id_type=MESH,
            )

        def lap(step, state):
            where = count - 1 - step if backward else step
            outbox[pl.ds(where, 1)] = state[None].astype(BF16)

            @pl.when(where != place)
            def _():
                returning(where).start()
                pltpu.make_async_remote_copy(
                    src_ref=part_ref.at[h],
                    dst_ref=inbox.at[where],
                    send_sem=send_sem.at[h],
                    recv_sem=recv_sem.at[where],
                    device_id=(group, where),
                    device_id_type=MESH,
                ).wait_recv()

            @pl.when(where == place)
            def _():
                landed[h : h + 1] = outbox[pl.ds(where, 1)]

            got = inbox[pl.ds(where, 1)][0]
            high, low = halves(state)
            if backward:
                step_map = maps_ref[pl.ds(where, 1)][0][:, width:]
                state = mm(step_map, high, TN) + mm(step_map, low, TN) + got.astype(F32)
            else:
                step_map = got[:, width:]
                state = mm(step_map, high) + mm(step_map, low) + got[:, :width].astype(F32)
            return state

        lax.fori_loop(0, count, lap, jnp.zeros((width, width), F32))

        def finish(where, carry):
            @pl.when(where != place)
            def _():
                returning(where).wait_send()

            return carry

        lax.fori_loop(0, count, finish, 0)

    for h in range(heads):

        @pl.when(place == keeper(h))
        def _(h=h):
            scan_head(h)

    for h in range(heads):

        @pl.when(place != keeper(h))
        def _(h=h):
            outgoing(h).wait_send()
            pltpu.make_async_remote_copy(
                src_ref=outbox.at[0],
                dst_ref=landed.at[h],
                send_sem=back_sem.at[0],
                recv_sem=land_sem.at[h],
                device_id=(group, keeper(h)),
                device_id_type=MESH,
            ).wait_recv()

    result_ref[...] = landed[...]
    if not backward:
        maps_ref[...] = inbox[...]


def carry_states(part, maps, count):
    heads, width, columns = part.shape
    backward = maps is not None
    out = jax.ShapeDtypeStruct
    vmem = pl.BlockSpec(memory_space=pltpu.VMEM)
    result = out((heads, width, width), BF16)
    return pl.pallas_call(
        partial(carry_kernel, count, heads, backward),
        in_specs=[vmem] * (2 if backward else 1),
        out_specs=vmem if backward else [vmem, vmem],
        out_shape=result if backward else [result, out((count, width, columns), BF16)],
        scratch_shapes=[
            pltpu.VMEM((count, width, columns), BF16),
            pltpu.VMEM((count, width, width), BF16),
            pltpu.VMEM((heads, width, width), BF16),
            pltpu.SemaphoreType.DMA((heads,)),
            pltpu.SemaphoreType.DMA((count,)),
            pltpu.SemaphoreType.DMA((count,)),
            pltpu.SemaphoreType.DMA((heads,)),
        ],
        compiler_params=pltpu.CompilerParams(
            collective_id=1 if backward else 0, has_side_effects=True, vmem_limit_bytes=VMEM_LIMIT
        ),
        name="carry_backward" if backward else "carry_forward",
    )(*((part, maps) if backward else (part,)))


def seq_positions(extras, first, total_rows):
    sizes = extras + (SHORTEST - 1)
    ends = jnp.cumsum(sizes)
    starts = ends - sizes
    row_ids = first + jnp.arange(total_rows, dtype=jnp.int32)
    inside = (row_ids[:, None] >= starts[None, :]) & (row_ids[:, None] < ends[None, :])
    return row_ids - jnp.sum(jnp.where(inside, starts[None, :], 0), axis=1)


def rms_scale(field, gain, epsilon):
    return field * lax.rsqrt(jnp.mean(field * field, axis=-1, keepdims=True) + epsilon) * gain


def rms_pull(field, gain, grad):
    scale = lax.rsqrt(jnp.mean(field * field, axis=-1, keepdims=True) + 1e-06)
    unit = field * scale
    through = grad * gain
    pulled = scale * (through - unit * jnp.mean(unit * through, axis=-1, keepdims=True))
    return pulled, jnp.sum(grad * unit, axis=0)


def dot32(a, b, dims=NN):
    return lax.dot_general(a, b, dims, preferred_element_type=F32)


def digits_of(count):
    radices = {16: (4, 2, 2), 128: (4, 4, 8)}.get(count)
    if radices is None:
        radices = ()
        left = count
        while left > 1:
            step = 4 if left % 4 == 0 else 2
            radices = radices + (step,)
            left = left // step
    return radices


def split_digits(index, radices):
    digits = []
    for radix in reversed(radices):
        digits.append(index % radix)
        index = index // radix
    return digits[::-1]


def join_digits(digits, radices):
    index = 0
    for digit, radix in zip(digits, radices):
        index = index * radix + digit
    return index


def relative_places(order, radices):
    here = split_digits(lax.axis_index("seq"), radices)
    count = 1
    for radix in radices:
        count *= radix
    place = jnp.arange(count, dtype=jnp.int32)
    moved = split_digits(place, [radices[axis] for axis in order])
    target = [None] * len(radices)
    for axis, move in zip(order, moved):
        target[axis] = (here[axis] + move) % radices[axis]
    return join_digits(target, radices)


def axis_shift(value, axis, move, radices):
    count = 1
    for radix in radices:
        count *= radix
    route = []
    for index in range(count):
        digits = split_digits(index, radices)
        digits[axis] = (digits[axis] + move) % radices[axis]
        route.append((index, join_digits(digits, radices)))
    return lax.ppermute(value, "seq", route)


def swap_core(value):
    count = lax.axis_size("dp")
    return lax.ppermute(value, "dp", [(i, (i + 1) % count) for i in range(count)])


def selector(depth, order, radices, group):
    places = relative_places(order, radices)
    count = places.shape[0]
    block = depth // (lax.axis_size("dp") * count)
    half = depth // lax.axis_size("dp")
    rows = (places[:, None] * block + jnp.arange(block, dtype=jnp.int32)).reshape(-1)
    source = group * half + rows
    return (jnp.arange(depth, dtype=jnp.int32)[:, None] == source[None, :]).astype(BF16)


def shard_sums(make, order, radices):
    count = 1
    for radix in radices:
        count *= radix
    first = count // radices[order[0]]
    arrived = [
        axis_shift(make(move * first, (move + 1) * first), order[0], move, radices)
        for move in range(1, radices[order[0]])
    ]
    total = make(0, first).astype(F32)
    for part in arrived:
        total = total + part.astype(F32)
    for axis in order[1:]:
        own = total.shape[0] // radices[axis]
        low = total.astype(BF16)
        arrived = [
            axis_shift(low[move * own : (move + 1) * own], axis, move, radices)
            for move in range(1, radices[axis])
        ]
        total = total[:own]
        for part in arrived:
            total = total + part.astype(F32)
    return total


def everywhere(value, radices):
    value = value + swap_core(value)
    for axis, radix in enumerate(radices):
        total = value
        if radix == 2:
            total = total + axis_shift(value, axis, 1, radices)
        else:
            step = 1
            while step < radix:
                total = total + exchange(total, axis, step, radices)
                step = 2 * step
        value = total
    return value


def exchange(value, axis, step, radices):
    count = 1
    for radix in radices:
        count *= radix
    route = []
    for index in range(count):
        digits = split_digits(index, radices)
        digits[axis] = digits[axis] ^ step
        route.append((index, join_digits(digits, radices)))
    return lax.ppermute(value, "seq", route)


def per_device(
    block_input, lengths, attn_gain, w_query, w_key, w_value, w_outgate, w_beta, w_decay, beta_bias,
    decay_rate, conv_query, conv_key, conv_value, out_gain, w_out, mlp_gain, w_gate, w_up, w_down,
    out_grad,
):
    rows, depth = block_input.shape
    heads = decay_rate.shape[0]
    width = out_gain.shape[0]
    blocks = rows // BLOCK
    count = lax.axis_size("seq")
    seq = lax.axis_index("seq")
    group = lax.axis_index("dp")
    radices = digits_of(count)
    axes = len(radices)
    order_a = tuple(range(axes - 1, -1, -1))
    order_b = (order_a[1], order_a[0]) + order_a[2:]
    places = seq_positions(lengths[0], seq * rows, rows)

    halo = lax.ppermute(block_input[rows - HALO :], "seq", [(i, i + 1) for i in range(count - 1)])
    xf = block_input.astype(F32)
    normed_b = rms_scale(xf, attn_gain, 1e-06).astype(BF16)
    ext_b = jnp.concatenate([rms_scale(halo.astype(F32), attn_gain, 1e-06).astype(BF16), normed_b], axis=0)
    rates = dot32(normed_b, jnp.concatenate([w_beta, w_decay], axis=1))
    beta_pre, decay_pre = rates[:, : heads * REFLECTS], rates[:, heads * REFLECTS :]
    betas = jax.nn.sigmoid(beta_pre + beta_bias)
    log_rate = jnp.where((places == 0)[:, None], RESET_LOG, -decay_rate * jax.nn.softplus(decay_pre))
    tri = jnp.tril(jnp.ones((BLOCK, BLOCK), F32))
    cumul = jnp.einsum(
        "ts,bsh->hbt", tri, log_rate.reshape(blocks, BLOCK, heads), precision=lax.Precision.HIGHEST
    )
    cumul = jnp.concatenate([cumul] * REFLECTS, axis=-1)
    beta_steps = betas.reshape(blocks, BLOCK, heads, REFLECTS).transpose(2, 0, 3, 1).reshape(heads, blocks, STEPS)
    arow = jnp.stack([cumul, beta_steps] + [jnp.zeros_like(cumul)] * 6, axis=2)
    acol = arow.transpose(0, 1, 3, 2)
    live = (places[:, None] >= jnp.arange(8, dtype=jnp.int32)[None, :]).astype(F32)
    taps = (conv_query, conv_key, conv_value)

    pre, gate_pre, oloc, oread, inv, delta, state, maps = mixer_forward(
        ext_b, w_query, w_key, w_value, w_outgate, taps, live, acol, arow, heads, width
    )
    start, all_maps = carry_states(maps, None, count)
    out_all, gated_b = gated_forward(oloc, oread, start, gate_pre, out_gain)

    resid = xf + dot32(gated_b, w_out)
    mlp_b = rms_scale(resid, mlp_gain, 1e-06).astype(BF16)
    gate_act = dot32(mlp_b, w_gate)
    up_act = dot32(mlp_b, w_up)
    gate_sig = jax.nn.sigmoid(gate_act)
    hidden_b = (gate_act * gate_sig * up_act).astype(BF16)
    block_output = (resid + dot32(hidden_b, w_down)).astype(BF16)
    d_hidden = dot32(out_grad, w_down, NT)
    d_gate_b = (d_hidden * up_act * (gate_sig + gate_act * gate_sig * (1.0 - gate_sig))).astype(BF16)
    d_up_b = (d_hidden * gate_act * gate_sig).astype(BF16)
    d_mlp = dot32(d_gate_b, w_gate, NT) + dot32(d_up_b, w_up, NT)
    d_resid_mlp, grad_mlp_gain = rms_pull(resid, mlp_gain, d_mlp)
    d_resid = out_grad.astype(F32) + d_resid_mlp
    d_branch_b = d_resid.astype(BF16)
    d_gated = dot32(d_branch_b, w_out, NT)
    d_out, d_outgate_b, part, grad_out_gain = gated_backward(out_all, gate_pre, out_gain, d_gated, oread)

    mine, other = selector(depth, order_a, radices, group), selector(depth, order_a, radices, 1 - group)

    def both(lhs, rhs):
        keep = dot32(lhs, mine).astype(BF16)
        gone = swap_core(dot32(lhs, other).astype(BF16))
        return jnp.concatenate([keep, gone], axis=0), jnp.concatenate([rhs, swap_core(rhs)], axis=0)

    first, second = radices[order_a[0]], radices[order_a[1]]

    def turned(lhs):
        tokens = lhs.shape[0]
        return lhs.reshape(tokens, first, second, -1).swapaxes(1, 2).reshape(tokens, -1)

    def maker(pairs):
        def make(begin, end):
            parts = []
            for lhs, rhs in pairs:
                block = lhs.shape[1] // count
                parts.append(dot32(lhs[:, begin * block : end * block], rhs, TN).astype(BF16))
            return parts[0] if len(parts) == 1 else jnp.concatenate(parts, axis=1)

        return make

    normed_l, outgate_r = both(normed_b, d_outgate_b)
    mlp_l, gate_r = both(mlp_b, d_gate_b)
    up_r = jnp.concatenate([d_up_b, swap_core(d_up_b)], axis=0)
    branch_l, gated_r = both(d_branch_b, gated_b)
    down_l, hidden_r = both(out_grad, hidden_b)
    early_a = shard_sums(maker([(mlp_l, gate_r), (branch_l, gated_r), (normed_l, outgate_r)]), order_a, radices)
    early_b = shard_sums(maker([(turned(mlp_l), up_r), (turned(down_l), hidden_r)]), order_b, radices)

    after = carry_states(part, all_maps, count)
    d_query, d_key, d_value, rim_q, rim_k, rim_v, tap_q, tap_k, tap_v, aux = mixer_backward(
        pre, taps, live, acol, arow, inv, delta, state, start, after, d_out
    )
    rim = lax.ppermute(
        jnp.concatenate([rim_q, rim_k, rim_v], axis=1), "seq", [(i, i - 1) for i in range(1, count)]
    )

    def settle(main, low):
        last = main[rows - HALO :].astype(F32) + low.astype(F32)
        return jnp.concatenate([main[: rows - HALO], last.astype(BF16)], axis=0)

    columns = heads * width
    d_query = settle(d_query, rim[:, :columns])
    d_key = settle(d_key, rim[:, columns : 3 * columns])
    d_value = settle(d_value, rim[:, 3 * columns :])
    d_beta = aux[:, :, :, 0].reshape(heads, blocks, REFLECTS, BLOCK).transpose(1, 3, 0, 2).reshape(rows, -1)
    d_log = jnp.einsum(
        "st,hbs->bth", tri, aux[:, :, :BLOCK, 1], precision=lax.Precision.HIGHEST
    ).reshape(rows, heads)
    d_log = jnp.where((places == 0)[:, None], 0.0, d_log)
    grad_decay_rate = jnp.sum(-jax.nn.softplus(decay_pre) * d_log, axis=0)
    d_decay = -decay_rate * jax.nn.sigmoid(decay_pre) * d_log
    grad_beta_bias = jnp.sum(d_beta, axis=0)
    d_rates_b = jnp.concatenate([d_beta, d_decay], axis=1).astype(BF16)

    rates_r = jnp.concatenate([d_rates_b, swap_core(d_rates_b)], axis=0)
    query_r = jnp.concatenate([d_query, swap_core(d_query)], axis=0)
    key_r = jnp.concatenate([d_key, swap_core(d_key)], axis=0)
    value_r = jnp.concatenate([d_value, swap_core(d_value)], axis=0)
    half = columns // 2
    late_a = shard_sums(
        maker([(normed_l, jnp.concatenate([key_r, query_r[:, :half]], axis=1))]), order_a, radices
    )
    late_b = shard_sums(
        maker([(turned(normed_l), jnp.concatenate([value_r, query_r[:, half:], rates_r], axis=1))]),
        order_b,
        radices,
    )

    d_normed = (
        dot32(d_query, w_query, NT)
        + dot32(d_key, w_key, NT)
        + dot32(d_value, w_value, NT)
        + dot32(d_outgate_b, w_outgate, NT)
        + dot32(d_rates_b, jnp.concatenate([w_beta, w_decay], axis=1), NT)
    )
    d_input_norm, grad_attn_gain = rms_pull(xf, attn_gain, d_normed)
    input_grad = (d_resid + d_input_norm).astype(BF16)

    small = [
        tap_q.reshape(-1),
        tap_k.reshape(-1),
        tap_v.reshape(-1),
        jnp.sum(grad_out_gain, axis=(0, 1)),
        grad_attn_gain,
        grad_mlp_gain,
        grad_beta_bias,
        grad_decay_rate,
    ]
    sizes = [piece.shape[0] for piece in small]
    flat = jnp.concatenate(small)
    lanes = 1024
    padded = jnp.pad(flat, (0, -flat.shape[0] % (8 * lanes))).reshape(-1, lanes)
    summed = everywhere(padded, radices).reshape(-1)
    pieces, begin = [], 0
    for size in sizes:
        pieces.append(summed[begin : begin + size])
        begin += size
    share = depth // (count * lax.axis_size("dp"))
    own = (group * count + seq) * share

    ff = w_gate.shape[1]
    return (
        block_output,
        input_grad,
        lax.dynamic_slice(pieces[4], (own,), (share,)),
        jnp.concatenate([late_a[:, 2 * columns :], late_b[:, 2 * columns : 2 * columns + half]], axis=1),
        late_a[:, : 2 * columns],
        late_b[:, : 2 * columns],
        early_a[:, ff + columns :],
        late_b[:, 2 * columns + half : 2 * columns + half + heads * REFLECTS],
        late_b[:, 2 * columns + half + heads * REFLECTS :],
        pieces[6],
        pieces[7],
        pieces[0].reshape(KW, -1),
        pieces[1].reshape(KW, -1),
        pieces[2].reshape(KW, -1),
        pieces[3],
        early_a[:, ff : ff + columns].T,
        lax.dynamic_slice(pieces[5], (own,), (share,)),
        early_a[:, :ff],
        early_b[:, :ff],
        early_b[:, ff:].T,
    )


def solution(mesh):
    tokens = P(("dp", "seq"), None)
    column = P(None, ("dp", "seq"))
    vector = P(("dp", "seq"))
    in_specs = (tokens, P("dp", None)) + (P(),) * 18 + (tokens,)
    out_specs = (
        (tokens, tokens, vector)
        + (tokens,) * 6
        + (P(),) * 6
        + (column, vector, tokens, tokens, column)
    )
    return jax.shard_map(
        per_device, mesh=mesh, in_specs=in_specs, out_specs=out_specs, check_vma=False
    )
```

time: 1890 us -> 519 us (0.27)
  waiting for transfers between devices: 863 us -> 157 us
  other arithmetic: 398 us -> 32.1 us
  matrix products: 317 us -> 76.6 us
  local copies, waits for them, and re-layouts: 267 us -> 45.1 us
  Pallas kernels: 0 us -> 142 us
  starting transfers between devices: 16.2 us -> 56.7 us
    reduce_scatter x1 -> x0, waiting for transfers between devices: 577 us -> none  [per_device(): lax.psum_scatter(jnp.concatenate([jnp.concatenate([trunk_gain_column, con...]
    another operation x13 -> x3, other arithmetic: 330 us -> 0.95 us  [the longest x1 0.76 us: per_device(): arow = jnp.stack([cumul, beta_steps] + [jnp.zeros_like(cumul)] * 6, axis=2)]
    dot_general x98 -> x38, matrix products: 301 us -> 76.6 us  [the longest x36 76.3 us: dot32(): return lax.dot_general(a, b, dims, preferred_element_type=F32)]
    all_gather x4 -> x0, waiting for transfers between devices: 166 us -> none  [the longest x2 118 us: prefix_2(): lax.all_gather(a.astype(kind), axis)]
    ppermute x6 -> x40, waiting for transfers between devices: 0.65 us -> 157 us  [the longest x22 149 us: axis_shift(): return lax.ppermute(value, 'seq', route)]
    pallas_call x0 -> x6, Pallas kernels: none -> 142 us  [the longest x2 52.2 us: carry_states(): pl.pallas_call(partial(carry_kernel, count, heads, backward), in_specs=[v...]
    psum x1 -> x0, waiting for transfers between devices: 120 us -> none  [per_device(): lax.psum((grad_conv_query, grad_conv_key, grad_conv_value, grad_out_gain,...]
    concatenate x2 -> x5, local copies, waits for them, and re-layouts: 74.6 us -> 3.17 us  [the longest x2 2.96 us: both(): jnp.concatenate([rhs, swap_core(rhs)], axis=0)]
  transfers between devices with their start and end apart: 12 -> 40, of which waited for: 6 -> 14; matrix products, arithmetic and copies ran while one was open for 13% -> 29% of each run, Pallas kernels for 0% -> 28%
where the time goes in v1:
time: 519 us; the launch traced here: 511 us
  waiting for transfers between devices  157 us (30%)
  Pallas kernels  142 us (27%)
  matrix products  76.6 us (15%)
  starting transfers between devices  56.7 us (11%)
  local copies, waits for them, and re-layouts  45.1 us (9%)
  other arithmetic  32.1 us (6%)
    ppermute x22, waiting for transfers between devices, axis_shift(): return lax.ppermute(value, 'seq', route)  149 us
    dot_general x36, matrix products, dot32(): return lax.dot_general(a, b, dims, preferred_element_type=F32)  76.3 us
    pallas_call x2, Pallas kernels, carry_states(): pl.pallas_call(partial(carry_kernel, count, heads, backward), in_specs=[v...  52.2 us
    ppermute x22, starting transfers between devices, axis_shift(): return lax.ppermute(value, 'seq', route)  44.8 us
    pallas_call x1, Pallas kernels, mixer_forward(): pl.pallas_call(mixer_forward_kernel, grid=(heads,), in_specs=[whole((ext_...  40.9 us
    pallas_call x1, Pallas kernels, mixer_backward(): pl.pallas_call(mixer_backward_kernel, grid=(heads,), in_specs=[per_head(p...  34.9 us
  transfers between devices with their start and end apart: 40, of which 14 were waited for; matrix products, arithmetic and copies ran while one was open for 29% of the time, Pallas kernels for 28%

profile of v1, /device:TPU:0, one launch (start us, length us, event | category | flops | bytes accessed | tf_op | source)
XLA Modules:
  0.0 511.3 jit_solution(5799900339041982781)
XLA Ops:
  1.6 4.8 collective-permute-start
  17.8 1.9 copy.130.acol_ref
  20.8 40.9 %mixer_forward.1 = (bf16[8,264,640]{2,1,0:T(8,128)(2,1)}, f32[256,1024]{1,0:T(8,128)}, f32[256,1024]{1,0:T(8,128)}, f32[8,256,128]{2,1,0:T(8,128)}, f32[8,4,128,...) custom-call(bf16[264,1024]{1,0:T(8,128)(2,1)} %pad_maximum_fusion.18.xn_, ...), custom_call_target="tpu_custom_call" | custom-call | tf_op jit(solution)/shard_map/mixer_forward/pallas_call | solution.py:183
  61.8 21.6 %carry_forward.1 = (bf16[8,128,128]{2,1,0:T(8,128)(2,1)}, bf16[16,128,256]{2,1,0:T(8,128)(2,1)}) custom-call(bf16[8,128,256]{2,1,0:T(8,128)(2,1)} %get-tuple-element.48.refs_0_), custom_call_target="tpu_custom_call" | custom-call | tf_op jit(solution)/shard_map/carry_forward/pallas_call | solution.py:587
  83.3 6.7 %gated_forward.1 = (f32[256,1024]{1,0:T(8,128)}, bf16[256,1024]{1,0:T(8,128)(2,1)}) custom-call(f32[256,1024]{1,0:T(8,128)} %get-tuple-element.46.oloc_ref, f32[8,256,128]{2,1,0:T(8,128)} %get-tuple-element.47.oread_ref, bf16[8,128,128]{2,1,0:T(8,128)(2,1)} %get-tuple-element.49.start_ref, f32[256,1024]{1,0:T(8,128)} %get-tuple-element.50.gate_ref, ...), custom_call_target="tpu_custom_call" | custom-call | tf_op jit(solution)/shard_map/gated_forward/pallas_call | solution.py:397
  92.1 6.6 %fusion.139 = f32[256,2816]{1,0:T(8,128)} fusion(bf16[256,1024]{1,0:T(8,128)(2,1)S(1)} %multiply_convert_fusion.3, bf16[1024,2816]{1,0:T(8,128)(2,1)} %param.38), kind=kOutput, calls=%fused_computation.269 | convolution fusion | flops 1476395008 | bytes 9175040 | tf_op jit(solution)/shard_map/dot_general | solution.py:630
  98.7 3.2 fusion.140
  101.9 5.8 %multiply_convert_fusion = (bf16[256,2816]{1,0:T(8,128)(2,1)S(1)}, bf16[256,2816]{1,0:T(8,128)(2,1)S(1)}, bf16[256,2816]{1,0:T(8,128)(2,1)}) fusion(f32[256,2816]{1,0:T(8,128)} %fusion.139, f32[256,2816]{1,0:T(8,128)} %fusion.140, bf16[256,1024]{1,0:T(8,128)(2,1)S(1)} %copy-done.28, bf16[2816,1024]{1,0:T(8,128)(2,1)S(1)} %bitcast.133), kind=kOutput, calls=%fused_computation.22 | convolution fusion | flops 1487208448 | bytes 16384000 | tf_op jit(solution)/shard_map/dot_general | solution.py:630
  114.4 7.1 %gated_backward.1 = (f32[256,1024]{1,0:T(8,128)}, bf16[256,1024]{1,0:T(8,128)(2,1)}, bf16[8,128,128]{2,1,0:T(8,128)(2,1)}, f32[8,1,128]{2,1,0:T(1,128)}) custom-call(f32[256,1024]{1,0:T(8,128)} %get-tuple-element.56.out_ref, f32[256,1024]{1,0:T(8,128)} %get-tuple-element.50.gate_ref, f32[1,128]{1,0:T(1,128)} %bitcast.126, f32[256,1024]{1,0:T(8,128)} %fusion.113.dgated_ref, ...), custom_call_target="tpu_custom_call" | custom-call | tf_op jit(solution)/shard_map/gated_backward/pallas_call | solution.py:435
  121.5 30.7 %carry_backward.1.after_ref = bf16[8,128,128]{2,1,0:T(8,128)(2,1)} custom-call(bf16[8,128,128]{2,1,0:T(8,128)(2,1)} %get-tuple-element.57.refs_0_, bf16[16,128,256]{2,1,0:T(8,128)(2,1)} %get-tuple-element.58.refs_1_), custom_call_target="tpu_custom_call" | custom-call | tf_op jit(solution)/shard_map/carry_backward/pallas_call | solution.py:587
  152.1 34.9 %mixer_backward.1 = (bf16[256,1024]{1,0:T(8,128)(2,1)}, bf16[256,2048]{1,0:T(8,128)(2,1)}, bf16[256,2048]{1,0:T(8,128)(2,1)}, bf16[8,1024]{1,0:T(8,128)(2,1)}, b...) custom-call(bf16[8,264,640]{2,1,0:T(8,128)(2,1)} %get-tuple-element., ...), custom_call_target="tpu_custom_call" | custom-call | tf_op jit(solution)/shard_map/mixer_backward/pallas_call | solution.py:335
  187.1 2.7 slice.231
  189.8 2.2 copy.132
  198.1 5.3 %fusion.20 = bf16[256,1024]{1,0:T(8,128)(2,1)} fusion(f32[256,1024]{1,0:T(8,128)S(1)} %copy-done.4, bf16[256,2816]{1,0:T(8,128)(2,1)S(1)} %copy-done.56, bf16[2816,1024]{1,0:T(8,128)(2,1)} %param.40), kind=kOutput, calls=%fused_computation.62 | convolution fusion | flops 1476919296 | bytes 8781824 | tf_op jit(solution)/shard_map/dot_general | solution.py:630
  209.4 2.4 slice.227
  215.2 3.9 fusion.124
  229.1 2.3 collective-permute-start.3
  232.4 2.1 collective-permute-done.3
  238.8 4.1 collective-permute-done.4
  244.4 2.3 collective-permute-start.5
  252.1 1.9 constant_dynamic-update-slice_fusion.4
  254.0 2.7 convolution_convert_fusion.10
  258.0 2.1 convolution_convert_fusion.12
  261.9 3.3 collective-permute-done.6
  271.6 2.6 convolution_convert_fusion.6
  274.7 2.3 convolution_convert_fusion.8
  278.2 2.4 convolution_convert_fusion.4
  283.1 2.4 convolution_convert_fusion
  289.9 3.5 convolution_convert_fusion.2
  293.4 2.0 convolution_convert_fusion.3
  295.4 13.3 %collective-permute-done.10 = bf16[256,2560]{1,0:T(8,128)(2,1)S(1)} collective-permute-done((bf16[256,2560]{1,0:T(8,128)(2,1)S(1)}, bf16[256,2560]{1,0:T(8,128)(2,1)S(1)}, u32[]{:S(2)}, u32[]{:S(2)}) %collective-permute-start.10) | collective-permute-done | bytes 1310752 | tf_op jit(solution)/shard_map/ppermute | solution.py:682
  308.7 2.2 fusion.3
  312.7 3.5 convolution_convert_fusion.5
  316.2 2.5 fusion.1
  319.1 61.9 %collective-permute-done.11 = bf16[128,2560]{1,0:T(8,128)(2,1)S(1)} collective-permute-done((bf16[128,2560]{1,0:T(8,128)(2,1)S(1)}, bf16[128,2560]{1,0:T(8,128)(2,1)S(1)}, u32[]{:S(2)}, u32[]{:S(2)}) %collective-permute-start.11) | collective-permute-done | bytes 655392 | tf_op jit(solution)/shard_map/ppermute | solution.py:682
  390.2 2.7 collective-permute-start.21
  392.8 5.7 %collective-permute-done.13 = bf16[32,2560]{1,0:T(8,128)(2,1)} collective-permute-done((bf16[32,2560]{1,0:T(8,128)(2,1)}, bf16[32,2560]{1,0:T(8,128)(2,1)}, u32[]{:S(2)}, u32[]{:S(2)}) %collective-permute-start.13) | collective-permute-done | bytes 163872 | tf_op jit(solution)/shard_map/ppermute | solution.py:682
  398.6 7.6 %collective-permute-start.19 = (bf16[32,2584]{1,0:T(8,128)(2,1)S(1)}, bf16[32,2584]{1,0:T(8,128)(2,1)}, u32[]{:S(2)}, u32[]{:S(2)}) collective-permute-start(bf16[32,2584]{1,0:T(8,128)(2,1)S(1)} %copy.138), channel_id=1, source_target_pairs={{0,4},{1,5},{2,6},{3,7},{4,8},{5,9},{6,10},{7,11},{8,12},{9,13},{1... | collective-permute-start | bytes 496136 | tf_op jit(solution)/shard_map/ppermute | solution.py:682
  408.6 3.5 collective-permute-done.20
  417.1 2.4 convert_add_fusion.1
  420.9 2.6 convert_add_fusion
  424.1 24.0 %collective-permute-done.28 = bf16[128,4864]{1,0:T(8,128)(2,1)S(1)} collective-permute-done((bf16[128,4864]{1,0:T(8,128)(2,1)S(1)}, bf16[128,4864]{1,0:T(8,128)(2,1)S(1)}, u32[]{:S(2)}, u32[]{:S(2)}) %collective-permute-start.28) | collective-permute-done | bytes 1245216 | tf_op jit(solution)/shard_map/ppermute | solution.py:682
  448.4 4.9 collective-permute-start.31
  454.4 1.9 collective-permute-done.36
  456.8 4.9 collective-permute-start.39
  461.6 11.4 %collective-permute-start.37 = (bf16[32,5632]{1,0:T(8,128)(2,1)S(1)}, bf16[32,5632]{1,0:T(8,128)(2,1)S(1)}, u32[]{:S(2)}, u32[]{:S(2)}) collective-permute-start(bf16[32,5632]{1,0:T(8,128)(2,1)S(1)} %get-tuple-element.209), channel_id=1, source_target_pairs={{0,4},{1,5},{2,6},{3,7},{4,8},{5,9},{6,10},{7,11},{8,12},{9,13},{1... | collective-permute-start | bytes 1081352 | tf_op jit(solution)/shard_map/ppermute | solution.py:682
  473.1 8.8 %collective-permute-done.30 = bf16[32,4864]{1,0:T(8,128)(2,1)S(1)} collective-permute-done((bf16[32,4864]{1,0:T(8,128)(2,1)S(1)}, bf16[32,4864]{1,0:T(8,128)(2,1)S(1)}, u32[]{:S(2)}, u32[]{:S(2)}) %collective-permute-start.30) | collective-permute-done | bytes 311328 | tf_op jit(solution)/shard_map/ppermute | solution.py:682
  483.5 26.5 %collective-permute-done.38 = bf16[32,5632]{1,0:T(8,128)(2,1)S(1)} collective-permute-done((bf16[32,5632]{1,0:T(8,128)(2,1)S(1)}, bf16[32,5632]{1,0:T(8,128)(2,1)S(1)}, u32[]{:S(2)}, u32[]{:S(2)}) %collective-permute-start.38) | collective-permute-done | bytes 360480 | tf_op jit(solution)/shard_map/ppermute | solution.py:682
  (353 shorter events, 102.3 us)
Async XLA Ops:
  0.7 89.3 %copy-start = (bf16[1024,1024]{1,0:T(8,128)(2,1)S(1)}, bf16[1024,1024]{1,0:T(8,128)(2,1)}, u32[]{:S(2)}) copy-start(bf16[1024,1024]{1,0:T(8,128)(2,1)} %param.36) | copy-start | bytes 6291460
  0.7 9.8 %copy-start.28 = (bf16[256,1024]{1,0:T(8,128)(2,1)S(1)}, bf16[256,1024]{1,0:T(8,128)(2,1)}, u32[]{:S(2)}) copy-start(bf16[256,1024]{1,0:T(8,128)(2,1)} %param.41) | copy-start | bytes 1572868
  1.6 18.2 %collective-permute-start = (bf16[8,1024]{1,0:T(8,128)(2,1)S(1)}, bf16[8,1024]{1,0:T(8,128)(2,1)S(1)}, u32[]{:S(2)}, u32[]{:S(2)}) collective-permute-start(bf16[8,1024]{1,0:T(8,128)(2,1)S(1)} %slice.218), channel_id=1, source_target_pairs={{0,1},{1,2},{2,3},{3,4},{4,5},{5,6},{6,7},{7,8},{8,9},{9,10},{10,1... | collective-permute-start | bytes 49160 | tf_op jit(solution)/shard_map/ppermute | solution.py:770
  10.4 218.7 %collective-permute-start.7 = (bf16[256,512]{1,0:T(8,128)(2,1)}, bf16[256,512]{1,0:T(8,128)(2,1)}, u32[]{:S(2)}, u32[]{:S(2)}) collective-permute-start(bf16[256,512]{1,0:T(8,128)(2,1)} %fusion.25), channel_id=1, source_target_pairs={{0,16},{16,0},{1,17},{17,1},{2,18},{18,2},{3,19},{19,3},{4,20},{20... | collective-permute-start | bytes 786440 | tf_op jit(solution)/shard_map/ppermute | solution.py:687
  11.8 222.8 %collective-permute-start.33 = (bf16[256,512]{1,0:T(8,128)(2,1)}, bf16[256,512]{1,0:T(8,128)(2,1)}, u32[]{:S(2)}, u32[]{:S(2)}) collective-permute-start(bf16[256,512]{1,0:T(8,128)(2,1)} %fusion.29), channel_id=1, source_target_pairs={{0,16},{16,0},{1,17},{17,1},{2,18},{18,2},{3,19},{19,3},{4,20},{20... | collective-permute-start | bytes 786440 | tf_op jit(solution)/shard_map/ppermute | solution.py:687
  61.7 28.2 %copy-start.2 = (bf16[256,1024]{1,0:T(8,128)(2,1)S(1)}, bf16[256,1024]{1,0:T(8,128)(2,1)}, u32[]{:S(2)}) copy-start(bf16[256,1024]{1,0:T(8,128)(2,1)} %param.21) | copy-start | bytes 1572868
  91.8 19.5 %copy-start.3 = (f32[256,1024]{1,0:T(8,128)}, f32[256,1024]{1,0:T(8,128)S(1)}, u32[]{:S(2)}) copy-start(f32[256,1024]{1,0:T(8,128)S(1)} %get-tuple-element.240) | copy-start | bytes 3145732
  91.9 10.0 %slice-start.5 = ((s8[5767168]{0:T(1024)(128)(4,1)}), s8[4194304]{0:T(1024)(128)(4,1)S(1)}, s32[]{:S(2)}) async-start(s8[5767168]{0:T(1024)(128)(4,1)} %bitcast.132), calls=%async_computation.5 | async-start | bytes 8388608
  92.1 9.8 %slice-start.6 = ((s8[5767168]{0:T(1024)(128)(4,1)}), s8[1572864]{0:T(1024)(128)(4,1)S(1)}, s32[]{:S(2)}) async-start(s8[5767168]{0:T(1024)(128)(4,1)} %bitcast.132), calls=%async_computation.6 | async-start | bytes 3145728
  205.5 8.0 %collective-permute-start.16 = (bf16[256,24]{0,1:T(8,128)(2,1)S(1)}, bf16[256,24]{0,1:T(8,128)(2,1)S(1)}, u32[]{:S(2)}, u32[]{:S(2)}) collective-permute-start(bf16[256,24]{0,1:T(8,128)(2,1)S(1)} %pad_maximum_fusion.29), channel_id=1, source_target_pairs={{0,16},{16,0},{1,17},{17,1},{2,18},{18,2},{3,19},{19,3},{4,20},{20... | collective-permute-start | bytes 36872 | tf_op jit(solution)/shard_map/ppermute | solution.py:687
  205.6 46.1 %collective-permute-start.26 = (bf16[256,1024]{1,0:T(8,128)(2,1)S(1)}, bf16[256,1024]{1,0:T(8,128)(2,1)}, u32[]{:S(2)}, u32[]{:S(2)}) collective-permute-start(bf16[256,1024]{1,0:T(8,128)(2,1)S(1)} %copy-done.16), channel_id=1, source_target_pairs={{0,16},{16,0},{1,17},{17,1},{2,18},{18,2},{3,19},{19,3},{4,20},{20... | collective-permute-start | bytes 1572872 | tf_op jit(solution)/shard_map/ppermute | solution.py:687
  207.6 6.8 %collective-permute-start.1 = (bf16[8,5120]{1,0:T(8,128)(2,1)}, bf16[8,5120]{1,0:T(8,128)(2,1)}, u32[]{:S(2)}, u32[]{:S(2)}) collective-permute-start(bf16[8,5120]{1,0:T(8,128)(2,1)} %pad_maximum_fusion.26), channel_id=1, source_target_pairs={{1,0},{2,1},{3,2},{4,3},{5,4},{6,5},{7,6},{8,7},{9,8},{10,9},{11,1... | collective-permute-start | bytes 245768 | tf_op jit(solution)/shard_map/ppermute | solution.py:847
  213.6 30.8 %collective-permute-start.22 = (bf16[256,512]{1,0:T(8,128)(2,1)}, bf16[256,512]{1,0:T(8,128)(2,1)}, u32[]{:S(2)}, u32[]{:S(2)}) collective-permute-start(bf16[256,512]{1,0:T(8,128)(2,1)} %fusion.26), channel_id=1, source_target_pairs={{0,16},{16,0},{1,17},{17,1},{2,18},{18,2},{3,19},{19,3},{4,20},{20... | collective-permute-start | bytes 786440 | tf_op jit(solution)/shard_map/ppermute | solution.py:687
  227.6 1.4 collective-permute-start.2
  228.9 27.8 %collective-permute-start.25 = (bf16[256,1024]{1,0:T(8,128)(2,1)S(1)}, bf16[256,1024]{1,0:T(8,128)(2,1)}, u32[]{:S(2)}, u32[]{:S(2)}) collective-permute-start(bf16[256,1024]{1,0:T(8,128)(2,1)S(1)} %copy-done.15), channel_id=1, source_target_pairs={{0,16},{16,0},{1,17},{17,1},{2,18},{18,2},{3,19},{19,3},{4,20},{20... | collective-permute-start | bytes 1572872 | tf_op jit(solution)/shard_map/ppermute | solution.py:687
  229.1 5.4 %collective-permute-start.3 = (f32[24,1024]{1,0:T(8,128)S(1)}, f32[24,1024]{1,0:T(8,128)S(1)}, u32[]{:S(2)}, u32[]{:S(2)}) collective-permute-start(f32[24,1024]{1,0:T(8,128)S(1)} %add.421), channel_id=1, source_target_pairs={{0,4},{1,5},{2,6},{3,7},{4,0},{5,1},{6,2},{7,3},{8,12},{9,13},{10,... | collective-permute-start | bytes 294920 | tf_op jit(solution)/shard_map/ppermute | solution.py:749
  234.5 43.6 %collective-permute-start.23 = (bf16[256,2816]{1,0:T(8,128)(2,1)}, bf16[256,2816]{1,0:T(8,128)(2,1)}, u32[]{:S(2)}, u32[]{:S(2)}) collective-permute-start(bf16[256,2816]{1,0:T(8,128)(2,1)} %copy-done.52), channel_id=1, source_target_pairs={{0,16},{16,0},{1,17},{17,1},{2,18},{18,2},{3,19},{19,3},{4,20},{20... | collective-permute-start | bytes 4325384 | tf_op jit(solution)/shard_map/ppermute | solution.py:687
  234.6 8.3 %collective-permute-start.4 = (f32[24,1024]{1,0:T(8,128)S(1)}, f32[24,1024]{1,0:T(8,128)S(1)}, u32[]{:S(2)}, u32[]{:S(2)}) collective-permute-start(f32[24,1024]{1,0:T(8,128)S(1)} %add.422), channel_id=1, source_target_pairs={{0,8},{1,9},{2,10},{3,11},{4,12},{5,13},{6,14},{7,15},{8,0},{9,1},... | collective-permute-start | bytes 294920 | tf_op jit(solution)/shard_map/ppermute | solution.py:749
  243.5 39.6 %collective-permute-start.34 = (bf16[256,2816]{1,0:T(8,128)(2,1)}, bf16[256,2816]{1,0:T(8,128)(2,1)}, u32[]{:S(2)}, u32[]{:S(2)}) collective-permute-start(bf16[256,2816]{1,0:T(8,128)(2,1)} %get-tuple-element.208), channel_id=1, source_target_pairs={{0,16},{16,0},{1,17},{17,1},{2,18},{18,2},{3,19},{19,3},{4,20},{20... | collective-permute-start | bytes 4325384 | tf_op jit(solution)/shard_map/ppermute | solution.py:687
  244.4 7.0 %collective-permute-start.5 = (f32[24,1024]{1,0:T(8,128)S(1)}, f32[24,1024]{1,0:T(8,128)S(1)}, u32[]{:S(2)}, u32[]{:S(2)}) collective-permute-start(f32[24,1024]{1,0:T(8,128)S(1)} %add.423), channel_id=1, source_target_pairs={{0,2},{1,3},{2,0},{3,1},{4,6},{5,7},{6,4},{7,5},{8,10},{9,11},{10,... | collective-permute-start | bytes 294920 | tf_op jit(solution)/shard_map/ppermute | solution.py:682
  251.4 8.7 %collective-permute-start.24 = (bf16[256,512]{1,0:T(8,128)(2,1)}, bf16[256,512]{1,0:T(8,128)(2,1)S(1)}, u32[]{:S(2)}, u32[]{:S(2)}) collective-permute-start(bf16[256,512]{1,0:T(8,128)(2,1)} %fusion.27), channel_id=1, source_target_pairs={{0,16},{16,0},{1,17},{17,1},{2,18},{18,2},{3,19},{19,3},{4,20},{20... | collective-permute-start | bytes 786440 | tf_op jit(solution)/shard_map/ppermute | solution.py:687
  251.7 18.2 %collective-permute-start.9 = (bf16[256,1024]{1,0:T(8,128)(2,1)}, bf16[256,1024]{1,0:T(8,128)(2,1)}, u32[]{:S(2)}, u32[]{:S(2)}) collective-permute-start(bf16[256,1024]{1,0:T(8,128)(2,1)} %pad_maximum_fusion.19), channel_id=1, source_target_pairs={{0,16},{16,0},{1,17},{17,1},{2,18},{18,2},{3,19},{19,3},{4,20},{20... | collective-permute-start | bytes 1572872 | tf_op jit(solution)/shard_map/ppermute | solution.py:687
  256.7 14.9 %collective-permute-start.15 = (bf16[256,2048]{1,0:T(8,128)(2,1)}, bf16[256,2048]{1,0:T(8,128)(2,1)}, u32[]{:S(2)}, u32[]{:S(2)}) collective-permute-start(bf16[256,2048]{1,0:T(8,128)(2,1)} %pad_maximum_fusion.14), channel_id=1, source_target_pairs={{0,16},{16,0},{1,17},{17,1},{2,18},{18,2},{3,19},{19,3},{4,20},{20... | collective-permute-start | bytes 3145736 | tf_op jit(solution)/shard_map/ppermute | solution.py:687
  260.1 5.0 collective-permute-start.6
  261.9 9.7 %copy-start.11 = (bf16[248,2048]{1,0:T(8,128)(2,1)S(1)}, bf16[248,2048]{1,0:T(8,128)(2,1)}, u32[]{:S(2)}) copy-start(bf16[248,2048]{1,0:T(8,128)(2,1)} %slice.227) | copy-start | bytes 3047428
  265.2 9.5 %collective-permute-start.8 = (bf16[256,2048]{1,0:T(8,128)(2,1)}, bf16[256,2048]{1,0:T(8,128)(2,1)}, u32[]{:S(2)}, u32[]{:S(2)}) collective-permute-start(bf16[256,2048]{1,0:T(8,128)(2,1)} %pad_maximum_fusion.13), channel_id=1, source_target_pairs={{0,16},{16,0},{1,17},{17,1},{2,18},{18,2},{3,19},{19,3},{4,20},{20... | collective-permute-start | bytes 3145736 | tf_op jit(solution)/shard_map/ppermute | solution.py:687
  269.9 15.7 %collective-permute-start.32 = (bf16[256,2816]{1,0:T(8,128)(2,1)}, bf16[256,2816]{1,0:T(8,128)(2,1)S(1)}, u32[]{:S(2)}, u32[]{:S(2)}) collective-permute-start(bf16[256,2816]{1,0:T(8,128)(2,1)} %copy-done.54), channel_id=1, source_target_pairs={{0,16},{16,0},{1,17},{17,1},{2,18},{18,2},{3,19},{19,3},{4,20},{20... | collective-permute-start | bytes 4325384 | tf_op jit(solution)/shard_map/ppermute | solution.py:687
  274.2 42.0 %collective-permute-start.17 = (bf16[256,2584]{0,1:T(8,128)(2,1)S(1)}, bf16[256,2584]{0,1:T(8,128)(2,1)S(1)}, u32[]{:S(2)}, u32[]{:S(2)}) collective-permute-start(bf16[256,2584]{0,1:T(8,128)(2,1)S(1)} %convolution_convert_fusion.6), channel_id=1, source_target_pairs={{0,2},{1,3},{2,0},{3,1},{4,6},{5,7},{6,4},{7,5},{8,10},{9,11},{10,... | collective-permute-start | bytes 3969032 | tf_op jit(solution)/shard_map/ppermute | solution.py:682
  277.0 31.7 %collective-permute-start.10 = (bf16[256,2560]{1,0:T(8,128)(2,1)S(1)}, bf16[256,2560]{1,0:T(8,128)(2,1)S(1)}, u32[]{:S(2)}, u32[]{:S(2)}) collective-permute-start(bf16[256,2560]{1,0:T(8,128)(2,1)S(1)} %convolution_convert_fusion.8), channel_id=1, source_target_pairs={{0,1},{1,0},{2,3},{3,2},{4,5},{5,4},{6,7},{7,6},{8,9},{9,8},{10,11... | collective-permute-start | bytes 3932168 | tf_op jit(solution)/shard_map/ppermute | solution.py:682
  282.2 135.0 %collective-permute-start.27 = (bf16[256,4864]{1,0:T(8,128)(2,1)}, bf16[256,4864]{1,0:T(8,128)(2,1)}, u32[]{:S(2)}, u32[]{:S(2)}) collective-permute-start(bf16[256,4864]{1,0:T(8,128)(2,1)} %pad_maximum_fusion.6), channel_id=1, source_target_pairs={{0,1},{1,0},{2,3},{3,2},{4,5},{5,4},{6,7},{7,6},{8,9},{9,8},{10,11... | collective-permute-start | bytes 7471112 | tf_op jit(solution)/shard_map/ppermute | solution.py:682
  288.3 132.5 %collective-permute-start.35 = (bf16[256,5632]{1,0:T(8,128)(2,1)}, bf16[256,5632]{1,0:T(8,128)(2,1)}, u32[]{:S(2)}, u32[]{:S(2)}) collective-permute-start(bf16[256,5632]{1,0:T(8,128)(2,1)} %pad_maximum_fusion.3), channel_id=1, source_target_pairs={{0,2},{1,3},{2,0},{3,1},{4,6},{5,7},{6,4},{7,5},{8,10},{9,11},{10,... | collective-permute-start | bytes 8650760 | tf_op jit(solution)/shard_map/ppermute | solution.py:682
  311.0 70.1 %collective-permute-start.11 = (bf16[128,2560]{1,0:T(8,128)(2,1)S(1)}, bf16[128,2560]{1,0:T(8,128)(2,1)S(1)}, u32[]{:S(2)}, u32[]{:S(2)}) collective-permute-start(bf16[128,2560]{1,0:T(8,128)(2,1)S(1)} %slice.465), channel_id=1, source_target_pairs={{0,2},{1,3},{2,0},{3,1},{4,6},{5,7},{6,4},{7,5},{8,10},{9,11},{10,... | collective-permute-start | bytes 1966088 | tf_op jit(solution)/shard_map/ppermute | solution.py:682
  318.8 64.7 %collective-permute-start.18 = (bf16[128,2584]{0,1:T(8,128)(2,1)S(1)}, bf16[128,2584]{0,1:T(8,128)(2,1)S(1)}, u32[]{:S(2)}, u32[]{:S(2)}) collective-permute-start(bf16[128,2584]{0,1:T(8,128)(2,1)S(1)} %slice.464), channel_id=1, source_target_pairs={{0,1},{1,0},{2,3},{3,2},{4,5},{5,4},{6,7},{7,6},{8,9},{9,8},{10,11... | collective-permute-start | bytes 1984520 | tf_op jit(solution)/shard_map/ppermute | solution.py:682
  383.1 7.1 %collective-permute-start.14 = (bf16[32,2560]{1,0:T(8,128)(2,1)}, bf16[32,2560]{1,0:T(8,128)(2,1)}, u32[]{:S(2)}, u32[]{:S(2)}) collective-permute-start(bf16[32,2560]{1,0:T(8,128)(2,1)} %get-tuple-element.223), channel_id=1, source_target_pairs={{0,12},{1,13},{2,14},{3,15},{4,0},{5,1},{6,2},{7,3},{8,4},{9,5},{1... | collective-permute-start | bytes 491528 | tf_op jit(solution)/shard_map/ppermute | solution.py:682
  383.5 15.0 %collective-permute-start.13 = (bf16[32,2560]{1,0:T(8,128)(2,1)}, bf16[32,2560]{1,0:T(8,128)(2,1)}, u32[]{:S(2)}, u32[]{:S(2)}) collective-permute-start(bf16[32,2560]{1,0:T(8,128)(2,1)} %get-tuple-element.224), channel_id=1, source_target_pairs={{0,8},{1,9},{2,10},{3,11},{4,12},{5,13},{6,14},{7,15},{8,0},{9,1},... | collective-permute-start | bytes 491528 | tf_op jit(solution)/shard_map/ppermute | solution.py:682
  383.5 15.0 %collective-permute-start.12 = (bf16[32,2560]{1,0:T(8,128)(2,1)}, bf16[32,2560]{1,0:T(8,128)(2,1)}, u32[]{:S(2)}, u32[]{:S(2)}) collective-permute-start(bf16[32,2560]{1,0:T(8,128)(2,1)} %get-tuple-element.222), channel_id=1, source_target_pairs={{0,4},{1,5},{2,6},{3,7},{4,8},{5,9},{6,10},{7,11},{8,12},{9,13},{1... | collective-permute-start | bytes 491528 | tf_op jit(solution)/shard_map/ppermute | solution.py:682
  390.2 18.0 %collective-permute-start.21 = (bf16[32,2584]{1,0:T(8,128)(2,1)S(1)}, bf16[32,2584]{1,0:T(8,128)(2,1)S(1)}, u32[]{:S(2)}, u32[]{:S(2)}) collective-permute-start(bf16[32,2584]{1,0:T(8,128)(2,1)S(1)} %copy.142), channel_id=1, source_target_pairs={{0,12},{1,13},{2,14},{3,15},{4,0},{5,1},{6,2},{7,3},{8,4},{9,5},{1... | collective-permute-start | bytes 496136 | tf_op jit(solution)/shard_map/ppermute | solution.py:682
  398.6 13.5 %collective-permute-start.20 = (bf16[32,2584]{1,0:T(8,128)(2,1)}, bf16[32,2584]{1,0:T(8,128)(2,1)S(1)}, u32[]{:S(2)}, u32[]{:S(2)}) collective-permute-start(bf16[32,2584]{1,0:T(8,128)(2,1)} %copy.140), channel_id=1, source_target_pairs={{0,8},{1,9},{2,10},{3,11},{4,12},{5,13},{6,14},{7,15},{8,0},{9,1},... | collective-permute-start | bytes 496136 | tf_op jit(solution)/shard_map/ppermute | solution.py:682
  398.6 13.9 %collective-permute-start.19 = (bf16[32,2584]{1,0:T(8,128)(2,1)S(1)}, bf16[32,2584]{1,0:T(8,128)(2,1)}, u32[]{:S(2)}, u32[]{:S(2)}) collective-permute-start(bf16[32,2584]{1,0:T(8,128)(2,1)S(1)} %copy.138), channel_id=1, source_target_pairs={{0,4},{1,5},{2,6},{3,7},{4,8},{5,9},{6,10},{7,11},{8,12},{9,13},{1... | collective-permute-start | bytes 496136 | tf_op jit(solution)/shard_map/ppermute | solution.py:682
  419.7 28.4 %collective-permute-start.28 = (bf16[128,4864]{1,0:T(8,128)(2,1)S(1)}, bf16[128,4864]{1,0:T(8,128)(2,1)S(1)}, u32[]{:S(2)}, u32[]{:S(2)}) collective-permute-start(bf16[128,4864]{1,0:T(8,128)(2,1)S(1)} %slice.463), channel_id=1, source_target_pairs={{0,2},{1,3},{2,0},{3,1},{4,6},{5,7},{6,4},{7,5},{8,10},{9,11},{10,... | collective-permute-start | bytes 3735560 | tf_op jit(solution)/shard_map/ppermute | solution.py:682
  423.7 32.6 %collective-permute-start.36 = (bf16[128,5632]{1,0:T(8,128)(2,1)S(1)}, bf16[128,5632]{1,0:T(8,128)(2,1)S(1)}, u32[]{:S(2)}, u32[]{:S(2)}) collective-permute-start(bf16[128,5632]{1,0:T(8,128)(2,1)S(1)} %slice.462), channel_id=1, source_target_pairs={{0,1},{1,0},{2,3},{3,2},{4,5},{5,4},{6,7},{7,6},{8,9},{9,8},{10,11... | collective-permute-start | bytes 4325384 | tf_op jit(solution)/shard_map/ppermute | solution.py:682
  448.4 13.3 %collective-permute-start.31 = (bf16[32,4864]{1,0:T(8,128)(2,1)S(1)}, bf16[32,4864]{1,0:T(8,128)(2,1)S(1)}, u32[]{:S(2)}, u32[]{:S(2)}) collective-permute-start(bf16[32,4864]{1,0:T(8,128)(2,1)S(1)} %get-tuple-element.213), channel_id=1, source_target_pairs={{0,12},{1,13},{2,14},{3,15},{4,0},{5,1},{6,2},{7,3},{8,4},{9,5},{1... | collective-permute-start | bytes 933896 | tf_op jit(solution)/shard_map/ppermute | solution.py:682
  453.2 28.6 %collective-permute-start.30 = (bf16[32,4864]{1,0:T(8,128)(2,1)S(1)}, bf16[32,4864]{1,0:T(8,128)(2,1)S(1)}, u32[]{:S(2)}, u32[]{:S(2)}) collective-permute-start(bf16[32,4864]{1,0:T(8,128)(2,1)S(1)} %get-tuple-element.214), channel_id=1, source_target_pairs={{0,8},{1,9},{2,10},{3,11},{4,12},{5,13},{6,14},{7,15},{8,0},{9,1},... | collective-permute-start | bytes 933896 | tf_op jit(solution)/shard_map/ppermute | solution.py:682
  453.2 28.6 %collective-permute-start.29 = (bf16[32,4864]{1,0:T(8,128)(2,1)S(1)}, bf16[32,4864]{1,0:T(8,128)(2,1)S(1)}, u32[]{:S(2)}, u32[]{:S(2)}) collective-permute-start(bf16[32,4864]{1,0:T(8,128)(2,1)S(1)} %get-tuple-element.212), channel_id=1, source_target_pairs={{0,4},{1,5},{2,6},{3,7},{4,8},{5,9},{6,10},{7,11},{8,12},{9,13},{1... | collective-permute-start | bytes 933896 | tf_op jit(solution)/shard_map/ppermute | solution.py:682
  456.8 26.7 %collective-permute-start.39 = (bf16[32,5632]{1,0:T(8,128)(2,1)S(1)}, bf16[32,5632]{1,0:T(8,128)(2,1)S(1)}, u32[]{:S(2)}, u32[]{:S(2)}) collective-permute-start(bf16[32,5632]{1,0:T(8,128)(2,1)S(1)} %get-tuple-element.210), channel_id=1, source_target_pairs={{0,12},{1,13},{2,14},{3,15},{4,0},{5,1},{6,2},{7,3},{8,4},{9,5},{1... | collective-permute-start | bytes 1081352 | tf_op jit(solution)/shard_map/ppermute | solution.py:682
  461.6 48.4 %collective-permute-start.38 = (bf16[32,5632]{1,0:T(8,128)(2,1)S(1)}, bf16[32,5632]{1,0:T(8,128)(2,1)S(1)}, u32[]{:S(2)}, u32[]{:S(2)}) collective-permute-start(bf16[32,5632]{1,0:T(8,128)(2,1)S(1)} %get-tuple-element.211), channel_id=1, source_target_pairs={{0,8},{1,9},{2,10},{3,11},{4,12},{5,13},{6,14},{7,15},{8,0},{9,1},... | collective-permute-start | bytes 1081352 | tf_op jit(solution)/shard_map/ppermute | solution.py:682
  461.6 48.4 %collective-permute-start.37 = (bf16[32,5632]{1,0:T(8,128)(2,1)S(1)}, bf16[32,5632]{1,0:T(8,128)(2,1)S(1)}, u32[]{:S(2)}, u32[]{:S(2)}) collective-permute-start(bf16[32,5632]{1,0:T(8,128)(2,1)S(1)} %get-tuple-element.209), channel_id=1, source_target_pairs={{0,4},{1,5},{2,6},{3,7},{4,8},{5,9},{6,10},{7,11},{8,12},{9,13},{1... | collective-permute-start | bytes 1081352 | tf_op jit(solution)/shard_map/ppermute | solution.py:682
  481.8 29.2 %copy-start.1 = (bf16[1024,1024]{1,0:T(8,128)(2,1)S(1)}, bf16[1024,1024]{1,0:T(8,128)(2,1)}, u32[]{:S(2)}) copy-start(bf16[1024,1024]{1,0:T(8,128)(2,1)} %param.36) | copy-start | bytes 6291460
  (59 other events, 264.4 us)

commit v2 on v1

--- a/solution.py
+++ b/solution.py
@@ -21,6 +21,12 @@
 NT = (((1,), (1,)), ((), ()))
 TN = (((0,), (0,)), ((), ()))
 VMEM_LIMIT = 56 * 1024 * 1024
+
+
+def cost(microseconds):
+    return pl.CostEstimate(
+        flops=int(microseconds * 1e9), bytes_accessed=int(microseconds * 1e6), transcendentals=0
+    )
 
 
 def mm(a, b, dims=NN):
@@ -218,6 +224,7 @@
         ],
         scratch_shapes=[pltpu.VMEM((ext_rows, 5 * width), F32)],
         compiler_params=pltpu.CompilerParams(vmem_limit_bytes=VMEM_LIMIT),
+        cost_estimate=cost(40),
         name="mixer_forward",
     )(xn, w_query, w_key, w_value, w_outgate, conv_query, conv_key, conv_value, live, acol, arow)
 
@@ -247,7 +254,7 @@
 def mixer_backward_kernel(
     pre_ref, tq_ref, tk_ref, tv_ref, live_ref, acol_ref, arow_ref,
     inv_ref, delta_ref, state_ref, start_ref, after_ref, dout_ref,
-    dq_ref, dk_ref, dv_ref, rimq_ref, rimk_ref, rimv_ref, dtq_ref, dtk_ref, dtv_ref, aux_ref,
+    d_ref, rim_ref, dtap_ref, aux_ref,
     ext_ref, pad_ref,
 ):
     rows, width = dout_ref.shape
@@ -308,17 +315,11 @@
     d_conv = [silu_pull(c, g) for c, g in zip(conv, d_act)]
     pad_ref[0:HALO, :] = jnp.zeros((HALO, width), F32)
     pad_ref[pl.ds(HALO + rows, HALO), :] = jnp.zeros((HALO, width), F32)
-    sides = (
-        (tq_ref, dq_ref, rimq_ref, dtq_ref, 0),
-        (tk_ref, dk_ref, rimk_ref, dtk_ref, 0),
-        (tk_ref, dk_ref, rimk_ref, dtk_ref, width),
-        (tv_ref, dv_ref, rimv_ref, dtv_ref, 0),
-        (tv_ref, dv_ref, rimv_ref, dtv_ref, width),
-    )
-    for i, (tap_ref, d_ref, rim_ref, dtap_ref, at) in enumerate(sides):
-        lanes = pl.ds(at, width)
+    sides = ((tq_ref, 0), (tk_ref, 0), (tk_ref, width), (tv_ref, 0), (tv_ref, width))
+    for i, (tap_ref, at) in enumerate(sides):
+        lanes = pl.ds(i * width, width)
         grad = conv_pull(
-            ext_ref, pad_ref, d_conv[i], tap_ref[:, lanes], live, pl.ds(i * width, width), rows,
+            ext_ref, pad_ref, d_conv[i], tap_ref[:, at : at + width], live, lanes, rows,
             dtap_ref.at[:, lanes],
         )
         rim_ref[:, lanes] = grad[:HALO].astype(BF16)
@@ -351,27 +352,15 @@
             head_columns(rows, width),
         ],
         out_specs=[
-            head_columns(rows, width),
-            head_columns(rows, 2 * width),
-            head_columns(rows, 2 * width),
-            head_columns(HALO, width),
-            head_columns(HALO, 2 * width),
-            head_columns(HALO, 2 * width),
-            head_columns(KW, width),
-            head_columns(KW, 2 * width),
-            head_columns(KW, 2 * width),
+            head_columns(rows, 5 * width),
+            head_columns(HALO, 5 * width),
+            head_columns(KW, 5 * width),
             per_head(acol.shape[1:]),
         ],
         out_shape=[
-            out((rows, columns), BF16),
-            out((rows, 2 * columns), BF16),
-            out((rows, 2 * columns), BF16),
-            out((HALO, columns), BF16),
-            out((HALO, 2 * columns), BF16),
-            out((HALO, 2 * columns), BF16),
-            out((KW, columns), F32),
-            out((KW, 2 * columns), F32),
-            out((KW, 2 * columns), F32),
+            out((rows, 5 * columns), BF16),
+            out((HALO, 5 * columns), BF16),
+            out((KW, 5 * columns), F32),
             out(acol.shape, F32),
         ],
         scratch_shapes=[
@@ -379,6 +368,7 @@
             pltpu.VMEM((rows + 2 * HALO, width), F32),
         ],
         compiler_params=pltpu.CompilerParams(vmem_limit_bytes=VMEM_LIMIT),
+        cost_estimate=cost(35),
         name="mixer_backward",
     )(pre, conv_query, conv_key, conv_value, live, acol, arow, inv, delta, state, start, after, dout)
 
@@ -406,6 +396,7 @@
         ],
         out_specs=[head_columns(rows, width), head_columns(rows, width)],
         out_shape=[out(oloc.shape, F32), out(oloc.shape, BF16)],
+        cost_estimate=cost(6),
         name="gated_forward",
     )(oloc, oread, start, gate_pre, out_gain[None, :])
 
@@ -454,6 +445,7 @@
             out((heads, width, width), BF16),
             out((heads, 1, width), F32),
         ],
+        cost_estimate=cost(6),
         name="gated_backward",
     )(out_all, gate_pre, out_gain[None, :], d_gated, oread)
 
@@ -601,9 +593,377 @@
         compiler_params=pltpu.CompilerParams(
             collective_id=1 if backward else 0, has_side_effects=True, vmem_limit_bytes=VMEM_LIMIT
         ),
+        cost_estimate=cost(24),
         name="carry_backward" if backward else "carry_forward",
     )(*((part, maps) if backward else (part,)))
 
+
+JOBS = 7
+JOB = 768
+LATE_JOBS = 10
+
+
+def row_blocks(parity, sending):
+    if sending:
+        return (1, 3) if parity else (2, 3)
+    return (0, 2) if parity else (0, 1)
+
+
+def early_products_kernel(own_ref, got_ref, *refs):
+    rhs_own, rhs_got, (send_a, send_b, keep_a, keep_b) = refs[:5], refs[5:10], refs[10:]
+    tokens = rhs_own[0].shape[0]
+    half = rhs_own[0].shape[1] // 2
+    edge = got_ref.shape[0] // 4
+    for parity, send_ref, keep_ref in ((0, send_a, keep_a), (1, send_b, keep_b)):
+        segments = [(0, 0, parity * half, half), (0, 1, parity * half, half), (1, 2, parity * half, half)]
+        segments.append((3, 4, 0, rhs_own[4].shape[1]) if parity else (2, 3, 0, rhs_own[3].shape[1]))
+        for out_ref, sending in ((send_ref, True), (keep_ref, False)):
+            at = 0
+            for lhs, rhs, begin, size in segments:
+                done = 0
+                while done < size:
+                    job, column = (at + done) // JOB, (at + done) % JOB
+                    width = min(JOB - column, size - done)
+                    lanes = slice(begin + done, begin + done + width)
+                    for row, block in enumerate(row_blocks(parity, sending)):
+                        rows = slice(block * edge, (block + 1) * edge)
+                        cut = slice(lhs * tokens, (lhs + 1) * tokens)
+                        total = mm(own_ref[rows, cut], rhs_own[rhs][:, lanes]) + mm(
+                            got_ref[rows, cut], rhs_got[rhs][:, lanes]
+                        )
+                        out_ref[job, row * edge : (row + 1) * edge, column : column + width] = total.astype(BF16)
+                    done += width
+                at += size
+
+
+def early_products(own, got, rhs_own, rhs_got):
+    rows = got.shape[0] // 2
+    shape = jax.ShapeDtypeStruct((JOBS, rows, JOB), BF16)
+    vmem = pl.BlockSpec(memory_space=pltpu.VMEM)
+    return pl.pallas_call(
+        early_products_kernel,
+        in_specs=[vmem] * 12,
+        out_specs=[vmem] * 4,
+        out_shape=[shape] * 4,
+        compiler_params=pltpu.CompilerParams(vmem_limit_bytes=VMEM_LIMIT),
+        cost_estimate=cost(10),
+        name="early_products",
+    )(own, got, *rhs_own, *rhs_got)
+
+
+def input_pull_kernel(
+    d_ref, rim_ref, dg_ref, rates_ref, wq_ref, wk_ref, wv_ref, wg_ref, wr_ref, x_ref, gain_ref, resid_ref,
+    settled_ref, grad_ref, dgain_ref, total_ref,
+):
+    head = pl.program_id(0)
+    rows = d_ref.shape[0]
+    width = wq_ref.shape[1]
+    last = d_ref[rows - HALO :, :].astype(F32) + rim_ref[...].astype(F32)
+    settled = jnp.concatenate([d_ref[: rows - HALO, :], last.astype(BF16)], axis=0)
+    settled_ref[...] = settled
+    part = (
+        mm(settled[:, :width], wq_ref[...], NT)
+        + mm(settled[:, width : 3 * width], wk_ref[...], NT)
+        + mm(settled[:, 3 * width :], wv_ref[...], NT)
+        + mm(dg_ref[...], wg_ref[...], NT)
+    )
+
+    @pl.when(head == 0)
+    def _():
+        total_ref[...] = part + mm(rates_ref[...], wr_ref[...], NT)
+
+    @pl.when(head > 0)
+    def _():
+        total_ref[...] += part
+
+    @pl.when(head == pl.num_programs(0) - 1)
+    def _():
+        x = x_ref[...].astype(F32)
+        grad = total_ref[...]
+        r = lax.rsqrt(jnp.mean(x * x, axis=-1, keepdims=True) + 1e-06)
+        unit = x * r
+        through = grad * gain_ref[...]
+        pulled = r * (through - unit * jnp.mean(unit * through, axis=-1, keepdims=True))
+        grad_ref[...] = (resid_ref[...] + pulled).astype(BF16)
+        dgain_ref[...] = jnp.sum(grad * unit, axis=0, keepdims=True)
+
+
+def input_pull(d_all, rim, d_outgate, d_rates, weights, w_rates, x, gain, d_resid, heads):
+    rows, depth = x.shape
+    width = d_outgate.shape[1] // heads
+    out = jax.ShapeDtypeStruct
+    w_query, w_key, w_value, w_outgate = weights
+    return pl.pallas_call(
+        input_pull_kernel,
+        grid=(heads,),
+        in_specs=[
+            head_columns(rows, 5 * width),
+            head_columns(HALO, 5 * width),
+            head_columns(rows, width),
+            whole(d_rates.shape),
+            head_columns(depth, width),
+            head_columns(depth, 2 * width),
+            head_columns(depth, 2 * width),
+            head_columns(depth, width),
+            whole(w_rates.shape),
+            whole(x.shape),
+            whole((1, depth)),
+            whole(d_resid.shape),
+        ],
+        out_specs=[head_columns(rows, 5 * width), whole(x.shape), whole((1, depth))],
+        out_shape=[out(d_all.shape, BF16), out(x.shape, BF16), out((1, depth), F32)],
+        scratch_shapes=[pltpu.VMEM((rows, depth), F32)],
+        compiler_params=pltpu.CompilerParams(vmem_limit_bytes=VMEM_LIMIT),
+        cost_estimate=cost(10),
+        name="input_pull",
+    )(d_all, rim, d_outgate, d_rates, w_query, w_key, w_value, w_outgate, w_rates, x, gain[None, :], d_resid)
+
+
+def reduce_kernel(
+    arr_a, arr_b, keep_a, keep_b, own_ref, got_ref, rhs_ref, small_ref,
+    early_ref, late_ref, total_ref,
+    e_keep2, e_send2, e_got2, e_keep3, e_send3, e_got3,
+    rhs_got, l_send1, l_got1, l_keep2, l_send2, l_got2, l_keep3, l_send3, l_got3, small_got,
+    dp_sem, e_sem2, e_sem3, l_sem1, l_sem2, l_sem3, s_sem,
+):
+    seq = lax.axis_index("seq")
+    group = lax.axis_index("dp")
+    x, y, z = seq % 2, (seq // 2) % 2, seq // 4
+    peers = (seq + 1 - 2 * x, seq + 2 - 4 * y)
+
+    def above(move):
+        return ((z + move) % 4) * 4 + seq % 4
+
+    core = {"dp": 1 - group, "seq": seq}
+
+    def at(place):
+        return {"dp": group, "seq": place}
+
+    def send(source, target, sems, index, device):
+        return pltpu.make_async_remote_copy(
+            src_ref=source,
+            dst_ref=target,
+            send_sem=sems.at[(0,) + index],
+            recv_sem=sems.at[(1,) + index],
+            device_id=device,
+            device_id_type=MESH,
+        )
+
+    barrier = pltpu.get_barrier_semaphore()
+    everyone = [core, at(peers[0]), at(peers[1])] + [at(above(move)) for move in (1, 2, 3)]
+    for device in everyone:
+        pl.semaphore_signal(barrier, inc=1, device_id=device, device_id_type=MESH)
+    pl.semaphore_wait(barrier, len(everyone))
+
+    swap = send(rhs_ref, rhs_got, dp_sem, (), core)
+    swap.start()
+
+    z1 = seq + 4 - 8 * (z % 2)
+    z2 = (z + 2 - 4 * (z // 2)) * 4 + seq % 4
+    hops = [core, at(peers[0]), at(peers[1]), at(z1), at(z2)]
+
+    def hop(step):
+        return send(total_ref.at[step], small_got.at[step], s_sem, (step,), hops[step])
+
+    def next_hop(step):
+        if step > 0:
+            hop(step - 1).wait_recv()
+            value = total_ref[step - 1] + small_got[step - 1]
+        else:
+            value = small_ref[...]
+        total_ref[step] = value
+        if step < len(hops):
+            hop(step).start()
+
+    next_hop(0)
+    keeps, arrs = (keep_a, keep_b), (arr_a, arr_b)
+    quarter = e_keep2.shape[2]
+    share = e_keep3.shape[2]
+
+    def copy2(p, i):
+        return send(e_send2.at[p, i], e_got2.at[p, i], e_sem2, (p, i), at(peers[1 - p]))
+
+    def copy3(p, i, move):
+        return send(
+            e_send3.at[p, i, pl.ds((move - 1) * share, share)],
+            e_got3.at[p, i, move - 1],
+            e_sem3,
+            (p, i, move - 1),
+            at(above(move)),
+        )
+
+    def early2(i, carry):
+        for p in range(2):
+            total = keeps[p][i].astype(F32) + arrs[p][i].astype(F32)
+            e_keep2[p, i] = total[:quarter].astype(BF16)
+            e_send2[p, i] = total[quarter:].astype(BF16)
+            copy2(p, i).start()
+        return carry
+
+    lax.fori_loop(0, JOBS, early2, 0)
+    next_hop(1)
+    swap.wait_recv()
+    job = l_got1.shape[-1]
+
+    def product(lhs, lanes, p, sending):
+        parts = []
+        for block in row_blocks(p, sending):
+            rows = pl.ds(block * quarter, quarter)
+            parts.append(mm(own_ref[rows, :], rhs_ref[:, lanes]) + mm(got_ref[rows, :], rhs_got[:, lanes]))
+        return parts
+
+    def lanes_of(m):
+        return pl.ds(pl.multiple_of(m * job, job), job)
+
+    def late_copy1(p, i):
+        return send(l_send1.at[p, i], l_got1.at[p, i], l_sem1, (p, i), at(peers[p]))
+
+    def late_copy2(p, i):
+        return send(l_send2.at[p, i], l_got2.at[p, i], l_sem2, (p, i), at(peers[1 - p]))
+
+    def late_copy3(p, i, move):
+        return send(
+            l_send3.at[p, i, pl.ds((move - 1) * share, share)],
+            l_got3.at[p, i, move - 1],
+            l_sem3,
+            (p, i, move - 1),
+            at(above(move)),
+        )
+
+    def late1(i, carry):
+        for p in range(2):
+            low, high = product(None, lanes_of(2 * i + p), p, True)
+            l_send1[p, i, 0:quarter] = low.astype(BF16)
+            l_send1[p, i, quarter : 2 * quarter] = high.astype(BF16)
+            late_copy1(p, i).start()
+        return carry
+
+    lax.fori_loop(0, LATE_JOBS // 2, late1, 0)
+    next_hop(2)
+
+    def early3(i, carry):
+        for p in range(2):
+            copy2(p, i).wait_recv()
+            total = e_keep2[p, i].astype(F32) + e_got2[p, i].astype(F32)
+            e_keep3[p, i] = total[:share].astype(BF16)
+            e_send3[p, i] = total[share:].astype(BF16)
+            for move in (1, 2, 3):
+                copy3(p, i, move).start()
+        return carry
+
+    lax.fori_loop(0, JOBS, early3, 0)
+    next_hop(3)
+
+    def late2(i, carry):
+        for p in range(2):
+            low, high = product(None, lanes_of(2 * i + p), p, False)
+            late_copy1(p, i).wait_recv()
+            l_keep2[p, i] = (low + l_got1[p, i, 0:quarter].astype(F32)).astype(BF16)
+            l_send2[p, i] = (high + l_got1[p, i, quarter : 2 * quarter].astype(F32)).astype(BF16)
+            late_copy2(p, i).start()
+        return carry
+
+    lax.fori_loop(0, LATE_JOBS // 2, late2, 0)
+    next_hop(4)
+
+    def early_end(i, carry):
+        for p in range(2):
+            total = e_keep3[p, i].astype(F32)
+            for move in (1, 2, 3):
+                copy3(p, i, move).wait_recv()
+                total = total + e_got3[p, i, move - 1].astype(F32)
+            early_ref[p, i] = total
+        return carry
+
+    lax.fori_loop(0, JOBS, early_end, 0)
+    next_hop(5)
+
+    def late3(i, carry):
+        for p in range(2):
+            late_copy2(p, i).wait_recv()
+            total = l_keep2[p, i].astype(F32) + l_got2[p, i].astype(F32)
+            l_keep3[p, i] = total[:share].astype(BF16)
+            l_send3[p, i] = total[share:].astype(BF16)
+            for move in (1, 2, 3):
+                late_copy3(p, i, move).start()
+        return carry
+
+    lax.fori_loop(0, LATE_JOBS // 2, late3, 0)
+
+    def late_end(i, carry):
+        for p in range(2):
+            total = l_keep3[p, i].astype(F32)
+            for move in (1, 2, 3):
+                late_copy3(p, i, move).wait_recv()
+                total = total + l_got3[p, i, move - 1].astype(F32)
+            late_ref[p, i] = total
+        return carry
+
+    lax.fori_loop(0, LATE_JOBS // 2, late_end, 0)
+
+    def early_sent(i, carry):
+        for p in range(2):
+            copy2(p, i).wait_send()
+            for move in (1, 2, 3):
+                copy3(p, i, move).wait_send()
+        return carry
+
+    def late_sent(i, carry):
+        for p in range(2):
+            late_copy1(p, i).wait_send()
+            late_copy2(p, i).wait_send()
+            for move in (1, 2, 3):
+                late_copy3(p, i, move).wait_send()
+        return carry
+
+    lax.fori_loop(0, JOBS, early_sent, 0)
+    lax.fori_loop(0, LATE_JOBS // 2, late_sent, 0)
+    swap.wait_send()
+    for step in range(len(hops)):
+        hop(step).wait_send()
+
+
+def reduce_all(arrived, kept, own, got, rhs, small):
+    half = kept[0].shape[1]
+    quarter, share = half // 2, half // 8
+    count = LATE_JOBS // 2
+    job = rhs.shape[1] // LATE_JOBS
+    out = jax.ShapeDtypeStruct
+    vmem = pl.BlockSpec(memory_space=pltpu.VMEM)
+    buffers = []
+    for jobs, width in ((JOBS, JOB), (count, job)):
+        if width == job:
+            buffers += [(rhs.shape, BF16), ((2, jobs, half, width), BF16), ((2, jobs, half, width), BF16)]
+        buffers += [((2, jobs, quarter, width), BF16)] * 3
+        buffers += [((2, jobs, share, width), BF16), ((2, jobs, 3 * share, width), BF16)]
+        buffers += [((2, jobs, 3, share, width), BF16)]
+    buffers += [((5,) + small.shape, F32)]
+    dma = pltpu.SemaphoreType.DMA
+    return pl.pallas_call(
+        reduce_kernel,
+        in_specs=[vmem] * 8,
+        out_specs=[vmem] * 3,
+        out_shape=[
+            out((2, JOBS, share, JOB), F32),
+            out((2, count, share, job), F32),
+            out((6,) + small.shape, F32),
+        ],
+        scratch_shapes=[pltpu.VMEM(shape, kind) for shape, kind in buffers]
+        + [
+            dma((2,)),
+            dma((2, 2, JOBS)),
+            dma((2, 2, JOBS, 3)),
+            dma((2, 2, count)),
+            dma((2, 2, count)),
+            dma((2, 2, count, 3)),
+            dma((2, 5)),
+        ],
+        compiler_params=pltpu.CompilerParams(
+            collective_id=2, has_side_effects=True, vmem_limit_bytes=VMEM_LIMIT
+        ),
+        cost_estimate=cost(90),
+        name="reduce_all",
+    )(*arrived, *kept, own, got, rhs, small)
 
 def seq_positions(extras, first, total_rows):
     sizes = extras + (SHORTEST - 1)
@@ -630,123 +990,29 @@
     return lax.dot_general(a, b, dims, preferred_element_type=F32)
 
 
-def digits_of(count):
-    radices = {16: (4, 2, 2), 128: (4, 4, 8)}.get(count)
-    if radices is None:
-        radices = ()
-        left = count
-        while left > 1:
-            step = 4 if left % 4 == 0 else 2
-            radices = radices + (step,)
-            left = left // step
-    return radices
-
-
-def split_digits(index, radices):
-    digits = []
-    for radix in reversed(radices):
-        digits.append(index % radix)
-        index = index // radix
-    return digits[::-1]
-
-
-def join_digits(digits, radices):
-    index = 0
-    for digit, radix in zip(digits, radices):
-        index = index * radix + digit
-    return index
-
-
-def relative_places(order, radices):
-    here = split_digits(lax.axis_index("seq"), radices)
-    count = 1
-    for radix in radices:
-        count *= radix
-    place = jnp.arange(count, dtype=jnp.int32)
-    moved = split_digits(place, [radices[axis] for axis in order])
-    target = [None] * len(radices)
-    for axis, move in zip(order, moved):
-        target[axis] = (here[axis] + move) % radices[axis]
-    return join_digits(target, radices)
-
-
-def axis_shift(value, axis, move, radices):
-    count = 1
-    for radix in radices:
-        count *= radix
-    route = []
-    for index in range(count):
-        digits = split_digits(index, radices)
-        digits[axis] = (digits[axis] + move) % radices[axis]
-        route.append((index, join_digits(digits, radices)))
-    return lax.ppermute(value, "seq", route)
-
-
 def swap_core(value):
     count = lax.axis_size("dp")
     return lax.ppermute(value, "dp", [(i, (i + 1) % count) for i in range(count)])
 
 
-def selector(depth, order, radices, group):
-    places = relative_places(order, radices)
-    count = places.shape[0]
-    block = depth // (lax.axis_size("dp") * count)
-    half = depth // lax.axis_size("dp")
-    rows = (places[:, None] * block + jnp.arange(block, dtype=jnp.int32)).reshape(-1)
-    source = group * half + rows
-    return (jnp.arange(depth, dtype=jnp.int32)[:, None] == source[None, :]).astype(BF16)
-
-
-def shard_sums(make, order, radices):
-    count = 1
-    for radix in radices:
-        count *= radix
-    first = count // radices[order[0]]
-    arrived = [
-        axis_shift(make(move * first, (move + 1) * first), order[0], move, radices)
-        for move in range(1, radices[order[0]])
-    ]
-    total = make(0, first).astype(F32)
-    for part in arrived:
-        total = total + part.astype(F32)
-    for axis in order[1:]:
-        own = total.shape[0] // radices[axis]
-        low = total.astype(BF16)
-        arrived = [
-            axis_shift(low[move * own : (move + 1) * own], axis, move, radices)
-            for move in range(1, radices[axis])
-        ]
-        total = total[:own]
-        for part in arrived:
-            total = total + part.astype(F32)
-    return total
-
-
-def everywhere(value, radices):
-    value = value + swap_core(value)
-    for axis, radix in enumerate(radices):
-        total = value
-        if radix == 2:
-            total = total + axis_shift(value, axis, 1, radices)
-        else:
-            step = 1
-            while step < radix:
-                total = total + exchange(total, axis, step, radices)
-                step = 2 * step
-        value = total
-    return value
-
-
-def exchange(value, axis, step, radices):
-    count = 1
-    for radix in radices:
-        count *= radix
-    route = []
-    for index in range(count):
-        digits = split_digits(index, radices)
-        digits[axis] = digits[axis] ^ step
-        route.append((index, join_digits(digits, radices)))
-    return lax.ppermute(value, "seq", route)
+def relative_selector(depth, group, seq):
+    block = depth // 32
+    index = jnp.arange(depth, dtype=jnp.int32)
+    row, place, side = index % block, (index // block) % 16, index // (16 * block)
+    x = (seq % 2) ^ (place // 8)
+    y = ((seq // 2) % 2) ^ ((place // 4) % 2)
+    z = (seq // 4 + place) % 4
+    source = (((group + side) % 2) * 16 + z * 4 + y * 2 + x) * block + row
+    return (index[:, None] == source[None, :]).astype(BF16)
+
+
+def neighbour_route(bit):
+    return [(i, i ^ bit) for i in range(16)]
+
+
+def by_head(field, heads, begin, size):
+    rows = field.shape[0]
+    return field.reshape(rows, heads, -1)[:, :, begin : begin + size].reshape(rows, heads * size)
 
 
 def per_device(
@@ -761,10 +1027,6 @@
     count = lax.axis_size("seq")
     seq = lax.axis_index("seq")
     group = lax.axis_index("dp")
-    radices = digits_of(count)
-    axes = len(radices)
-    order_a = tuple(range(axes - 1, -1, -1))
-    order_b = (order_a[1], order_a[0]) + order_a[2:]
     places = seq_positions(lengths[0], seq * rows, rows)
 
     halo = lax.ppermute(block_input[rows - HALO :], "seq", [(i, i + 1) for i in range(count - 1)])
@@ -809,53 +1071,27 @@
     d_gated = dot32(d_branch_b, w_out, NT)
     d_out, d_outgate_b, part, grad_out_gain = gated_backward(out_all, gate_pre, out_gain, d_gated, oread)
 
-    mine, other = selector(depth, order_a, radices, group), selector(depth, order_a, radices, 1 - group)
-
-    def both(lhs, rhs):
-        keep = dot32(lhs, mine).astype(BF16)
-        gone = swap_core(dot32(lhs, other).astype(BF16))
-        return jnp.concatenate([keep, gone], axis=0), jnp.concatenate([rhs, swap_core(rhs)], axis=0)
-
-    first, second = radices[order_a[0]], radices[order_a[1]]
-
-    def turned(lhs):
-        tokens = lhs.shape[0]
-        return lhs.reshape(tokens, first, second, -1).swapaxes(1, 2).reshape(tokens, -1)
-
-    def maker(pairs):
-        def make(begin, end):
-            parts = []
-            for lhs, rhs in pairs:
-                block = lhs.shape[1] // count
-                parts.append(dot32(lhs[:, begin * block : end * block], rhs, TN).astype(BF16))
-            return parts[0] if len(parts) == 1 else jnp.concatenate(parts, axis=1)
-
-        return make
-
-    normed_l, outgate_r = both(normed_b, d_outgate_b)
-    mlp_l, gate_r = both(mlp_b, d_gate_b)
-    up_r = jnp.concatenate([d_up_b, swap_core(d_up_b)], axis=0)
-    branch_l, gated_r = both(d_branch_b, gated_b)
-    down_l, hidden_r = both(out_grad, hidden_b)
-    early_a = shard_sums(maker([(mlp_l, gate_r), (branch_l, gated_r), (normed_l, outgate_r)]), order_a, radices)
-    early_b = shard_sums(maker([(turned(mlp_l), up_r), (turned(down_l), hidden_r)]), order_b, radices)
-
+    w_rates = jnp.concatenate([w_beta, w_decay], axis=1)
+    compact = count == 16
+    rhs_own = (d_gate_b, d_up_b, hidden_b, gated_b, d_outgate_b)
+    if compact:
+        rhs_got = tuple(swap_core(rhs) for rhs in rhs_own)
+        lhs = jnp.concatenate([mlp_b, out_grad, d_branch_b, normed_b], axis=0)
+        own_l = lax.dot_general(
+            relative_selector(depth, group, seq), lhs, (((0,), (1,)), ((), ())), preferred_element_type=F32
+        ).astype(BF16)
+        got_l = swap_core(own_l[depth // 2 :])
     after = carry_states(part, all_maps, count)
-    d_query, d_key, d_value, rim_q, rim_k, rim_v, tap_q, tap_k, tap_v, aux = mixer_backward(
+    if compact:
+        rhs_own, rhs_got, own_l, got_l, after = lax.optimization_barrier((rhs_own, rhs_got, own_l, got_l, after))
+        send_a, send_b, keep_a, keep_b = early_products(own_l, got_l, rhs_own, rhs_got)
+        arr_a = lax.ppermute(send_a, "seq", neighbour_route(1))
+        arr_b = lax.ppermute(send_b, "seq", neighbour_route(2))
+        after = lax.optimization_barrier((after, keep_a))[0]
+    d_all, rim, d_taps, aux = mixer_backward(
         pre, taps, live, acol, arow, inv, delta, state, start, after, d_out
     )
-    rim = lax.ppermute(
-        jnp.concatenate([rim_q, rim_k, rim_v], axis=1), "seq", [(i, i - 1) for i in range(1, count)]
-    )
-
-    def settle(main, low):
-        last = main[rows - HALO :].astype(F32) + low.astype(F32)
-        return jnp.concatenate([main[: rows - HALO], last.astype(BF16)], axis=0)
-
-    columns = heads * width
-    d_query = settle(d_query, rim[:, :columns])
-    d_key = settle(d_key, rim[:, columns : 3 * columns])
-    d_value = settle(d_value, rim[:, 3 * columns :])
+    rim = lax.ppermute(rim, "seq", [(i, i - 1) for i in range(1, count)])
     d_beta = aux[:, :, :, 0].reshape(heads, blocks, REFLECTS, BLOCK).transpose(1, 3, 0, 2).reshape(rows, -1)
     d_log = jnp.einsum(
         "st,hbs->bth", tri, aux[:, :, :BLOCK, 1], precision=lax.Precision.HIGHEST
@@ -865,75 +1101,80 @@
     d_decay = -decay_rate * jax.nn.sigmoid(decay_pre) * d_log
     grad_beta_bias = jnp.sum(d_beta, axis=0)
     d_rates_b = jnp.concatenate([d_beta, d_decay], axis=1).astype(BF16)
-
-    rates_r = jnp.concatenate([d_rates_b, swap_core(d_rates_b)], axis=0)
-    query_r = jnp.concatenate([d_query, swap_core(d_query)], axis=0)
-    key_r = jnp.concatenate([d_key, swap_core(d_key)], axis=0)
-    value_r = jnp.concatenate([d_value, swap_core(d_value)], axis=0)
-    half = columns // 2
-    late_a = shard_sums(
-        maker([(normed_l, jnp.concatenate([key_r, query_r[:, :half]], axis=1))]), order_a, radices
+    d_all, input_grad, grad_attn_gain = input_pull(
+        d_all, rim, d_outgate_b, d_rates_b, (w_query, w_key, w_value, w_outgate), w_rates,
+        block_input, attn_gain, d_resid, heads,
     )
-    late_b = shard_sums(
-        maker([(turned(normed_l), jnp.concatenate([value_r, query_r[:, half:], rates_r], axis=1))]),
-        order_b,
-        radices,
+    grad_rates = dot32(d_rates_b, normed_b, TN)
+    misc = jnp.concatenate([jnp.sum(grad_out_gain, axis=(0, 1)), grad_beta_bias, grad_decay_rate])
+    edge = misc.shape[0]
+    small = jnp.concatenate(
+        [
+            d_taps.reshape(-1, depth),
+            grad_attn_gain,
+            grad_mlp_gain[None],
+            jnp.pad(misc, (0, depth - edge))[None],
+            jnp.zeros((1, depth), F32),
+            grad_rates,
+        ],
+        axis=0,
     )
-
-    d_normed = (
-        dot32(d_query, w_query, NT)
-        + dot32(d_key, w_key, NT)
-        + dot32(d_value, w_value, NT)
-        + dot32(d_outgate_b, w_outgate, NT)
-        + dot32(d_rates_b, jnp.concatenate([w_beta, w_decay], axis=1), NT)
-    )
-    d_input_norm, grad_attn_gain = rms_pull(xf, attn_gain, d_normed)
-    input_grad = (d_resid + d_input_norm).astype(BF16)
-
-    small = [
-        tap_q.reshape(-1),
-        tap_k.reshape(-1),
-        tap_v.reshape(-1),
-        jnp.sum(grad_out_gain, axis=(0, 1)),
-        grad_attn_gain,
-        grad_mlp_gain,
-        grad_beta_bias,
-        grad_decay_rate,
-    ]
-    sizes = [piece.shape[0] for piece in small]
-    flat = jnp.concatenate(small)
-    lanes = 1024
-    padded = jnp.pad(flat, (0, -flat.shape[0] % (8 * lanes))).reshape(-1, lanes)
-    summed = everywhere(padded, radices).reshape(-1)
-    pieces, begin = [], 0
-    for size in sizes:
-        pieces.append(summed[begin : begin + size])
-        begin += size
-    share = depth // (count * lax.axis_size("dp"))
-    own = (group * count + seq) * share
-
+    devices = count * lax.axis_size("dp")
+    share = depth // devices
+    here = (group * count + seq) * share
+    columns = heads * width
     ff = w_gate.shape[1]
+    if compact:
+        early, late, totals = reduce_all(
+            (arr_a, arr_b), (keep_a, keep_b), own_l[: depth // 2, 3 * rows :], got_l[:, 3 * rows :], d_all, small
+        )
+        small = totals[-1]
+        early = [early[p].transpose(1, 0, 2).reshape(share, -1) for p in range(2)]
+        late = late.transpose(2, 1, 0, 3).reshape(share, -1)
+        half = ff // 2
+        sums = [
+            jnp.concatenate([early[0][:, :half], early[1][:, :half]], axis=1),
+            jnp.concatenate([early[0][:, half : 2 * half], early[1][:, half : 2 * half]], axis=1),
+            jnp.concatenate([early[0][:, 2 * half : 3 * half], early[1][:, 2 * half : 3 * half]], axis=1),
+            early[0][:, 3 * half : 3 * half + columns],
+            early[1][:, 3 * half : 3 * half + columns],
+        ]
+    else:
+        small = lax.psum(small, ("dp", "seq"))
+        pairs = zip((mlp_b, mlp_b, out_grad, d_branch_b, normed_b, normed_b), rhs_own + (d_all,))
+        sums = [
+            lax.psum_scatter(dot32(lhs, rhs, TN), ("dp", "seq"), scatter_dimension=0, tiled=True)
+            for lhs, rhs in pairs
+        ]
+        late = sums.pop()
+    taps_sum = small[: KW * 5].reshape(KW, -1)
+    own_small = lax.dynamic_slice(small[KW * 5 :], (0, here), (small.shape[0] - KW * 5, share))
+    misc = small[KW * 5 + 2]
+    marks = ((0, width), (width, 2 * width), (3 * width, 2 * width))
+    taps_out = [by_head(taps_sum, heads, begin, size) for begin, size in marks]
+    trunk = [by_head(late, heads, begin, size) for begin, size in marks]
+    rates_sum = own_small[4:].T
     return (
         block_output,
         input_grad,
-        lax.dynamic_slice(pieces[4], (own,), (share,)),
-        jnp.concatenate([late_a[:, 2 * columns :], late_b[:, 2 * columns : 2 * columns + half]], axis=1),
-        late_a[:, : 2 * columns],
-        late_b[:, : 2 * columns],
-        early_a[:, ff + columns :],
-        late_b[:, 2 * columns + half : 2 * columns + half + heads * REFLECTS],
-        late_b[:, 2 * columns + half + heads * REFLECTS :],
-        pieces[6],
-        pieces[7],
-        pieces[0].reshape(KW, -1),
-        pieces[1].reshape(KW, -1),
-        pieces[2].reshape(KW, -1),
-        pieces[3],
-        early_a[:, ff : ff + columns].T,
-        lax.dynamic_slice(pieces[5], (own,), (share,)),
-        early_a[:, :ff],
-        early_b[:, :ff],
-        early_b[:, ff:].T,
+        own_small[0],
+        trunk[0],
+        trunk[1],
+        trunk[2],
+        sums[4],
+        rates_sum[:, : heads * REFLECTS],
+        rates_sum[:, heads * REFLECTS :],
+        misc[width : width + heads * REFLECTS],
+        misc[width + heads * REFLECTS : edge],
+        taps_out[0],
+        taps_out[1],
+        taps_out[2],
+        misc[:width],
+        sums[3].T,
+        own_small[1],
+        sums[0],
+        sums[1],
+        sums[2].T,
     )
 
 

time: 519 us -> 424 us (0.82)
  Pallas kernels: 142 us -> 309 us
  waiting for transfers between devices: 157 us -> 16.1 us
  starting transfers between devices: 56.7 us -> 10.5 us
  matrix products: 76.6 us -> 32.7 us
  other arithmetic: 32.1 us -> 12.4 us
  local copies, waits for them, and re-layouts: 45.1 us -> 35.8 us
    pallas_call x0 -> x3, Pallas kernels: none -> 168 us  [the longest x1 142 us: reduce_all(): pl.pallas_call(reduce_kernel, in_specs=[vmem] * 8, out_specs=[vmem] * 3,...]
    ppermute x25 -> x3, waiting for transfers between devices: 156 us -> 16.1 us  [the longest x1 16.1 us: per_device(): rim = lax.ppermute(rim, 'seq', [(i, i - 1) for i in range(1, count)])]
    dot_general x36 -> x10, matrix products: 76.3 us -> 29.9 us  [dot32(): return lax.dot_general(a, b, dims, preferred_element_type=F32)]
    ppermute x25 -> x3, starting transfers between devices: 49 us -> 2.73 us  [the longest x1 1.53 us: per_device(): rim = lax.ppermute(rim, 'seq', [(i, i - 1) for i in range(1, count)])]
    concatenate x12 -> x2, other arithmetic: 12.6 us -> 0.98 us  [the longest x1 0.9 us: per_device(): jnp.concatenate([early[0][:, :half], early[1][:, :half]], axis=1)]
    add x13 -> x1, other arithmetic: 8.16 us -> 0.02 us  [relative_selector(): source = ((group + side) % 2 * 16 + z * 4 + y * 2 + x) * block + row]
    reshape x9 -> x3, local copies, waits for them, and re-layouts: 7.21 us -> 0.14 us  [the longest x2 0.09 us: per_device(): early = [early[p].transpose(1, 0, 2).reshape(share, -1) for p in range(2)]]
    slice x30 -> x16, local copies, waits for them, and re-layouts: 14 us -> 11 us  [the longest x1 1.67 us: per_device(): own_l[:depth // 2, 3 * rows:]]
  transfers between devices with their start and end apart: 40 -> 10, of which waited for: 14 -> 1; matrix products, arithmetic and copies ran while one was open for 29% -> 9% of each run, Pallas kernels for 28% -> 20%
where the time goes in v2:
time: 424 us; the launch traced here: 419 us
  Pallas kernels  309 us (73%)
  local copies, waits for them, and re-layouts  35.8 us (8%)
  matrix products  32.7 us (8%)
  waiting for transfers between devices  16.1 us (4%)
  other arithmetic  12.4 us (3%)
  starting transfers between devices  10.5 us (2%)
    pallas_call x1, Pallas kernels, reduce_all(): pl.pallas_call(reduce_kernel, in_specs=[vmem] * 8, out_specs=[vmem] * 3,...  142 us
    pallas_call x2, Pallas kernels, carry_states(): pl.pallas_call(partial(carry_kernel, count, heads, backward), in_specs=[v...  51.3 us
    pallas_call x1, Pallas kernels, mixer_forward(): pl.pallas_call(mixer_forward_kernel, grid=(heads,), in_specs=[whole((ext_...  40.9 us
    pallas_call x1, Pallas kernels, mixer_backward(): pl.pallas_call(mixer_backward_kernel, grid=(heads,), in_specs=[per_head(p...  35 us
    dot_general x10, matrix products, dot32(): return lax.dot_general(a, b, dims, preferred_element_type=F32)  29.9 us
    ppermute x1, waiting for transfers between devices, per_device(): rim = lax.ppermute(rim, 'seq', [(i, i - 1) for i in range(1, count)])  16.1 us
    pallas_call x1, Pallas kernels, input_pull(): pl.pallas_call(input_pull_kernel, grid=(heads,), in_specs=[head_columns(r...  13.7 us
    pallas_call x1, Pallas kernels, early_products(): pl.pallas_call(early_products_kernel, in_specs=[vmem] * 12, out_specs=[vm...  13.1 us
  transfers between devices with their start and end apart: 10, of which 1 were waited for; matrix products, arithmetic and copies ran while one was open for 9% of the time, Pallas kernels for 20%

profile of v2, /device:TPU:0, one launch (start us, length us, event | category | flops | bytes accessed | tf_op | source)
XLA Modules:
  0.0 418.6 jit_solution(10246677923170239787)
XLA Ops:
  0.7 0.9 slice.127
  1.5 5.0 %collective-permute-start = (bf16[8,1024]{1,0:T(8,128)(2,1)S(1)}, bf16[8,1024]{1,0:T(8,128)(2,1)S(1)}, u32[]{:S(2)}, u32[]{:S(2)}) collective-permute-start(bf16[8,1024]{1,0:T(8,128)(2,1)S(1)} %slice.127), channel_id=1, source_target_pairs={{0,1},{1,2},{2,3},{3,4},{4,5},{5,6},{6,7},{7,8},{8,9},{9,10},{10,1... | collective-permute-start | bytes 49160 | tf_op jit(solution)/shard_map/ppermute | solution.py:1032
  6.5 1.2 fusion.18
  10.1 0.8 constant_dynamic-update-slice_fusion.1
  10.9 1.2 fusion.20
  16.7 0.8 copy.90.wr_ref
  17.5 2.0 copy.83.acol_ref
  19.7 0.8 pad_maximum_fusion.xn_ref
  20.5 40.9 %mixer_forward.1 = (bf16[8,264,640]{2,1,0:T(8,128)(2,1)}, f32[256,1024]{1,0:T(8,128)}, f32[256,1024]{1,0:T(8,128)}, f32[8,256,128]{2,1,0:T(8,128)}, f32[8,4,128,...) custom-call(bf16[264,1024]{1,0:T(8,128)(2,1)} %pad_maximum_fusion.xn_ref, ...), custom_call_target="tpu_custom_call" | custom-call | flops 40000000000 | bytes 40000000 | tf_op jit(solution)/shard_map/mixer_forward/pallas_call | solution.py:189
  61.4 21.5 %carry_forward.1 = (bf16[8,128,128]{2,1,0:T(8,128)(2,1)}, bf16[16,128,256]{2,1,0:T(8,128)(2,1)}) custom-call(bf16[8,128,256]{2,1,0:T(8,128)(2,1)} %get-tuple-element.66.refs_0_), custom_call_target="tpu_custom_call" | custom-call | flops 24000000000 | bytes 24000000 | tf_op jit(solution)/shard_map/carry_forward/pallas_call | solution.py:579
  82.9 6.6 %gated_forward.1 = (f32[256,1024]{1,0:T(8,128)}, bf16[256,1024]{1,0:T(8,128)(2,1)}) custom-call(f32[256,1024]{1,0:T(8,128)} %get-tuple-element.64.oloc_ref, f32[8,256,128]{2,1,0:T(8,128)} %get-tuple-element.65.oread_ref, bf16[8,128,128]{2,1,0:T(8,128)(2,1)} %get-tuple-element.67.start_ref, f32[256,1024]{1,0:T(8,128)} %get-tuple-element.68.gate_ref, ...), custom_call_target="tpu_custom_call" | custom-call | flops 6000000000 | bytes 6000000 | tf_op jit(solution)/shard_map/gated_forward/pallas_call | solution.py:387
  89.6 2.2 multiply_reduce_fusion.2
  92.0 4.4 %fusion.83 = f32[256,2816]{1,0:T(8,128)S(1)} fusion(bf16[256,1024]{1,0:T(8,128)(2,1)S(1)} %multiply_convert_fusion.3, bf16[1024,2816]{1,0:T(8,128)(2,1)} %param.38), kind=kOutput, calls=%fused_computation.169 | convolution fusion | flops 1476395008 | bytes 9175040 | tf_op jit(solution)/shard_map/dot_general | solution.py:990
  96.5 3.3 fusion.84
  99.8 6.0 %multiply_convert_fusion = (bf16[256,2816]{1,0:T(8,128)(2,1)}, bf16[256,2816]{1,0:T(8,128)(2,1)}, bf16[256,2816]{1,0:T(8,128)(2,1)}) fusion(f32[256,2816]{1,0:T(8,128)S(1)} %fusion.83, f32[256,2816]{1,0:T(8,128)} %fusion.84, bf16[256,1024]{1,0:T(8,128)(2,1)S(1)} %copy-done.8, bf16[2816,1024]{1,0:T(8,128)(2,1)S(1)} %bitcast.143), kind=kOutput, calls=%fused_computation.2 | convolution fusion | flops 1487208448 | bytes 16384000 | tf_op jit(solution)/shard_map/dot_general | solution.py:990
  105.8 3.0 fusion.85
  108.9 1.6 collective-permute-start.1
  111.0 3.2 multiply_reduce_fusion
  114.3 1.3 fusion.77
  115.6 1.7 fusion.86.dgated_ref
  117.4 2.4 fusion.11.own_ref
  120.4 0.8 copy-done.7
  121.2 7.1 %gated_backward.1 = (f32[256,1024]{1,0:T(8,128)}, bf16[256,1024]{1,0:T(8,128)(2,1)}, bf16[8,128,128]{2,1,0:T(8,128)(2,1)}, f32[8,1,128]{2,1,0:T(1,128)}) custom-call(f32[256,1024]{1,0:T(8,128)} %get-tuple-element.74.out_ref, f32[256,1024]{1,0:T(8,128)} %get-tuple-element.68.gate_ref, f32[1,128]{1,0:T(1,128)} %bitcast.145, f32[256,1024]{1,0:T(8,128)} %fusion.86.dgated_ref, ...), custom_call_target="tpu_custom_call" | custom-call | flops 6000000000 | bytes 6000000 | tf_op jit(solution)/shard_map/gated_backward/pallas_call | solution.py:426
  128.3 29.9 %carry_backward.1.after_ref = bf16[8,128,128]{2,1,0:T(8,128)(2,1)} custom-call(bf16[8,128,128]{2,1,0:T(8,128)(2,1)} %get-tuple-element.76.refs_0_, bf16[16,128,256]{2,1,0:T(8,128)(2,1)} %get-tuple-element.77.refs_1_), custom_call_target="tpu_custom_call" | custom-call | flops 24000000000 | bytes 24000000 | tf_op jit(solution)/shard_map/carry_backward/pallas_call | solution.py:579
  158.3 5.5 %fusion.17 = bf16[256,1024]{1,0:T(8,128)(2,1)} fusion(f32[256,1024]{1,0:T(8,128)S(1)} %get-tuple-element.136, bf16[256,2816]{1,0:T(8,128)(2,1)} %get-tuple-element.83.refs_2_, bf16[2816,1024]{1,0:T(8,128)(2,1)} %param.40), kind=kOutput, calls=%fused_computation.22 | convolution fusion | flops 1476919296 | bytes 8781824 | tf_op jit(solution)/shard_map/dot_general | solution.py:990
  163.9 0.8 copy-done.19
  165.0 13.1 %early_products.1 = (bf16[7,256,768]{2,1,0:T(8,128)(2,1)}, bf16[7,256,768]{2,1,0:T(8,128)(2,1)}, bf16[7,256,768]{2,1,0:T(8,128)(2,1)}, bf16[7,256,768]{2,1,0:T(8,128)(2,1)}) custom-call(bf16[1024,1024]{1,0:T(8,128)(2,1)} %copy-done.7, bf16[512,1024]{1,0:T(8,128)(2,1)} %copy-done.11, bf16[256,2816]{1,0:T(8,128)(2,1)} %get-tuple-element.81.refs_0_, ...), custom_call_target="tpu_custom_call" | custom-call | flops 10000000000 | bytes 10000000 | tf_op jit(solution)/shard_map/early_products/pallas_call | solution.py:643
  178.0 1.1 collective-permute-start.8
  179.2 35.0 %mixer_backward.1 = (bf16[256,5120]{1,0:T(8,128)(2,1)}, bf16[8,5120]{1,0:T(8,128)(2,1)}, f32[4,5120]{1,0:T(4,128)}, f32[8,4,128,8]{3,2,1,0:T(8,128)}) custom-call(bf16[8,264,640]{2,1,0:T(8,128)(2,1)} %get-tuple-element.70.pre_ref, f32[4,1024]{1,0:T(4,128)} %tq_ref.3, f32[4,2048]{1,0:T(4,128)} %tk_ref.3, f32[4,2048]{1,0:T(4,128)} %tv_ref.3, ...), custom_call_target="tpu_custom_call" | custom-call | flops 35000000512 | bytes 35000000 | tf_op jit(solution)/shard_map/mixer_backward/pallas_call | solution.py:336
  214.3 1.7 slice.133.own_ref
  215.9 1.7 slice.134.got_ref
  217.6 1.5 collective-permute-start.7
  219.2 1.6 slice.132
  221.4 2.2 copy.85
  223.9 0.9 multiply_reduce_fusion.3
  226.0 16.1 %collective-permute-done.7.rim_ref = bf16[8,5120]{1,0:T(8,128)(2,1)S(1)} collective-permute-done((bf16[8,5120]{1,0:T(8,128)(2,1)}, bf16[8,5120]{1,0:T(8,128)(2,1)S(1)}, u32[]{:S(2)}, u32[]{:S(2)}) %collective-permute-start.7) | collective-permute-done | bytes 81952 | tf_op jit(solution)/shard_map/ppermute | solution.py:1094
  242.7 13.7 %input_pull.1 = (bf16[256,5120]{1,0:T(8,128)(2,1)}, bf16[256,1024]{1,0:T(8,128)(2,1)}, f32[1,1024]{1,0:T(1,128)}) custom-call(bf16[256,5120]{1,0:T(8,128)(2,1)} %get-tuple-element.94.d_ref, bf16[8,5120]{1,0:T(8,128)(2,1)} %copy-done.20, bf16[256,1024]{1,0:T(8,128)(2,1)} %get-tuple-element.85.refs_4_.dg_ref, bf16[256,24]{1,0:T(8,128)(2,1)} %copy.89.rates_ref, ...), custom_call_target="tpu_custom_call" | custom-call | flops 10000000000 | bytes 10000000 | tf_op jit(solution)/shard_map/input_pull/pallas_call | solution.py:696
  256.4 2.7 concatenate.38.small_ref
  259.1 141.8 %reduce_all.1 = (f32[2,7,32,768]{3,2,1,0:T(8,128)}, f32[2,5,32,512]{3,2,1,0:T(8,128)}, f32[6,48,1024]{2,1,0:T(8,128)}) custom-call(bf16[7,256,768]{2,1,0:T(8,128)(2,1)} %collective-permute-done.8.arr_a, bf16[7,256,768]{2,1,0:T(8,128)(2,1)} %collective-permute-done.9.arr_b, bf16[7,256,768]{2,1,0:T(8,128)(2,1)} %get-tuple-element.91.keep_a, ...), custom_call_target="tpu_custom_call" | custom-call | flops 89999998976 | bytes 90000000 | tf_op jit(solution)/shard_map/reduce_all/pallas_call | solution.py:942
  400.9 1.7 copy.91
  403.2 1.1 slice.135
  405.5 1.2 slice_bitcast_fusion.8
  406.7 1.3 slice_bitcast_fusion.7
  408.0 0.9 slice.150
  408.9 1.2 slice_bitcast_fusion.6
  413.1 0.8 copy.97
  413.9 0.8 copy.98
  417.3 0.9 pad_maximum_fusion.1
  (142 shorter events, 19.1 us)
Async XLA Ops:
  0.7 88.9 %copy-start = (bf16[1024,1024]{1,0:T(8,128)(2,1)S(1)}, bf16[1024,1024]{1,0:T(8,128)(2,1)}, u32[]{:S(2)}) copy-start(bf16[1024,1024]{1,0:T(8,128)(2,1)} %param.36) | copy-start | bytes 6291460
  1.5 18.1 %copy-start.13 = (f32[1024]{0:T(1024)S(1)}, f32[1024]{0:T(1024)}, u32[]{:S(2)}) copy-start(f32[1024]{0:T(1024)} %param.23) | copy-start | bytes 12292
  1.5 17.9 %collective-permute-start = (bf16[8,1024]{1,0:T(8,128)(2,1)S(1)}, bf16[8,1024]{1,0:T(8,128)(2,1)S(1)}, u32[]{:S(2)}, u32[]{:S(2)}) collective-permute-start(bf16[8,1024]{1,0:T(8,128)(2,1)S(1)} %slice.127), channel_id=1, source_target_pairs={{0,1},{1,2},{2,3},{3,4},{4,5},{5,6},{6,7},{7,8},{8,9},{9,10},{10,1... | collective-permute-start | bytes 49160 | tf_op jit(solution)/shard_map/ppermute | solution.py:1032
  9.4 5.4 %copy-start.14 = (pred[256]{0:T(512)(128)(4,1)}, pred[256]{0:T(512)(128)(4,1)S(1)}, u32[]{:S(2)}) copy-start(pred[256]{0:T(512)(128)(4,1)S(1)} %get-tuple-element.112) | copy-start | bytes 772
  12.1 49.3 %copy-start.2 = (bf16[256,1024]{1,0:T(8,128)(2,1)}, bf16[256,1024]{1,0:T(8,128)(2,1)S(1)}, u32[]{:S(2)}) copy-start(bf16[256,1024]{1,0:T(8,128)(2,1)S(1)} %fusion.20) | copy-start | bytes 1572868
  13.1 2.7 copy-start.9
  14.8 0.5 copy-start.17
  89.6 2.2 copy-start.12
  89.6 6.8 %slice-start.3 = ((s8[5767168]{0:T(1024)(128)(4,1)}), s8[4194304]{0:T(1024)(128)(4,1)S(1)}, s32[]{:S(2)}) async-start(s8[5767168]{0:T(1024)(128)(4,1)} %bitcast.140), calls=%async_computation.3 | async-start | bytes 8388608
  91.9 4.5 %slice-start.4 = ((s8[5767168]{0:T(1024)(128)(4,1)}), s8[1572864]{0:T(1024)(128)(4,1)S(1)}, s32[]{:S(2)}) async-start(s8[5767168]{0:T(1024)(128)(4,1)} %bitcast.140), calls=%async_computation.4 | async-start | bytes 3145728
  91.9 7.8 %slice-start.5 = ((s8[5767168]{0:T(1024)(128)(4,1)}), s8[4194304]{0:T(1024)(128)(4,1)S(1)}, s32[]{:S(2)}) async-start(s8[5767168]{0:T(1024)(128)(4,1)} %bitcast.142), calls=%async_computation.5 | async-start | bytes 8388608
  96.4 3.3 copy-start.8
  96.4 3.3 slice-start.6
  96.5 9.4 %slice-start.1 = ((s8[5767168]{0:T(1024)(128)(4,1)}), s8[4194304]{0:T(1024)(128)(4,1)S(1)}, s32[]{:S(2)}) async-start(s8[5767168]{0:T(1024)(128)(4,1)} %bitcast.138), calls=%async_computation.1 | async-start | bytes 8388608
  99.8 6.1 %slice-start.2 = ((s8[5767168]{0:T(1024)(128)(4,1)}), s8[1572864]{0:T(1024)(128)(4,1)S(1)}, s32[]{:S(2)}) async-start(s8[5767168]{0:T(1024)(128)(4,1)} %bitcast.138), calls=%async_computation.2 | async-start | bytes 3145728
  108.9 55.0 %collective-permute-start.1 = (bf16[256,2816]{1,0:T(8,128)(2,1)}, bf16[256,2816]{1,0:T(8,128)(2,1)}, u32[]{:S(2)}, u32[]{:S(2)}) collective-permute-start(bf16[256,2816]{1,0:T(8,128)(2,1)} %get-tuple-element.81.refs_0_), channel_id=1, source_target_pairs={{0,16},{16,0},{1,17},{17,1},{2,18},{18,2},{3,19},{19,3},{4,20},{20... | collective-permute-start | bytes 4325384 | tf_op jit(solution)/shard_map/ppermute | solution.py:995
  110.5 47.7 %collective-permute-start.4 = (bf16[256,1024]{1,0:T(8,128)(2,1)}, bf16[256,1024]{1,0:T(8,128)(2,1)}, u32[]{:S(2)}, u32[]{:S(2)}) collective-permute-start(bf16[256,1024]{1,0:T(8,128)(2,1)} %get-tuple-element.84.refs_3_), channel_id=1, source_target_pairs={{0,16},{16,0},{1,17},{17,1},{2,18},{18,2},{3,19},{19,3},{4,20},{20... | collective-permute-start | bytes 1572872 | tf_op jit(solution)/shard_map/ppermute | solution.py:995
  110.6 53.3 %collective-permute-start.2 = (bf16[256,2816]{1,0:T(8,128)(2,1)}, bf16[256,2816]{1,0:T(8,128)(2,1)}, u32[]{:S(2)}, u32[]{:S(2)}) collective-permute-start(bf16[256,2816]{1,0:T(8,128)(2,1)} %get-tuple-element.82.refs_1_), channel_id=1, source_target_pairs={{0,16},{16,0},{1,17},{17,1},{2,18},{18,2},{3,19},{19,3},{4,20},{20... | collective-permute-start | bytes 4325384 | tf_op jit(solution)/shard_map/ppermute | solution.py:995
  115.6 1.8 copy-start.3
  117.3 46.5 %collective-permute-start.3 = (bf16[256,2816]{1,0:T(8,128)(2,1)}, bf16[256,2816]{1,0:T(8,128)(2,1)}, u32[]{:S(2)}, u32[]{:S(2)}) collective-permute-start(bf16[256,2816]{1,0:T(8,128)(2,1)} %get-tuple-element.83.refs_2_), channel_id=1, source_target_pairs={{0,16},{16,0},{1,17},{17,1},{2,18},{18,2},{3,19},{19,3},{4,20},{20... | collective-permute-start | bytes 4325384 | tf_op jit(solution)/shard_map/ppermute | solution.py:995
  119.8 1.4 copy-start.7
  119.9 43.9 %collective-permute-start.6 = (bf16[512,1024]{1,0:T(8,128)(2,1)S(1)}, bf16[512,1024]{1,0:T(8,128)(2,1)S(1)}, u32[]{:S(2)}, u32[]{:S(2)}) collective-permute-start(bf16[512,1024]{1,0:T(8,128)(2,1)S(1)} %slice.167), channel_id=1, source_target_pairs={{0,16},{16,0},{1,17},{17,1},{2,18},{18,2},{3,19},{19,3},{4,20},{20... | collective-permute-start | bytes 3145736 | tf_op jit(solution)/shard_map/ppermute | solution.py:995
  128.3 29.9 %copy-start.16 = (f32[8,1,128]{2,1,0:T(1,128)S(1)}, f32[8,1,128]{2,1,0:T(1,128)}, u32[]{:S(2)}) copy-start(f32[8,1,128]{2,1,0:T(1,128)} %get-tuple-element.104) | copy-start | bytes 12292
  158.2 5.6 %collective-permute-start.5 = (bf16[256,1024]{1,0:T(8,128)(2,1)}, bf16[256,1024]{1,0:T(8,128)(2,1)S(1)}, u32[]{:S(2)}, u32[]{:S(2)}) collective-permute-start(bf16[256,1024]{1,0:T(8,128)(2,1)} %get-tuple-element.85.refs_4_.dg_ref), channel_id=1, source_target_pairs={{0,16},{16,0},{1,17},{17,1},{2,18},{18,2},{3,19},{19,3},{4,20},{20... | collective-permute-start | bytes 1572872 | tf_op jit(solution)/shard_map/ppermute | solution.py:995
  163.8 0.8 copy-start.19
  163.8 1.2 copy-start.11
  178.0 81.1 %collective-permute-start.8 = (bf16[7,256,768]{2,1,0:T(8,128)(2,1)}, bf16[7,256,768]{2,1,0:T(8,128)(2,1)}, u32[]{:S(2)}, u32[]{:S(2)}) collective-permute-start(bf16[7,256,768]{2,1,0:T(8,128)(2,1)} %get-tuple-element.98), channel_id=1, source_target_pairs={{0,1},{1,0},{2,3},{3,2},{4,5},{5,4},{6,7},{7,6},{8,9},{9,8},{10,11... | collective-permute-start | bytes 8257544 | tf_op jit(solution)/shard_map/ppermute | solution.py:1088
  179.1 80.0 %collective-permute-start.9 = (bf16[7,256,768]{2,1,0:T(8,128)(2,1)}, bf16[7,256,768]{2,1,0:T(8,128)(2,1)}, u32[]{:S(2)}, u32[]{:S(2)}) collective-permute-start(bf16[7,256,768]{2,1,0:T(8,128)(2,1)} %get-tuple-element.99), channel_id=1, source_target_pairs={{0,2},{1,3},{2,0},{3,1},{4,6},{5,7},{6,4},{7,5},{8,10},{9,11},{10,... | collective-permute-start | bytes 8257544 | tf_op jit(solution)/shard_map/ppermute | solution.py:1089
  217.6 24.5 %collective-permute-start.7 = (bf16[8,5120]{1,0:T(8,128)(2,1)}, bf16[8,5120]{1,0:T(8,128)(2,1)S(1)}, u32[]{:S(2)}, u32[]{:S(2)}) collective-permute-start(bf16[8,5120]{1,0:T(8,128)(2,1)} %get-tuple-element.95), channel_id=1, source_target_pairs={{1,0},{2,1},{3,2},{4,3},{5,4},{6,5},{7,6},{8,7},{9,8},{10,9},{11,1... | collective-permute-start | bytes 245768 | tf_op jit(solution)/shard_map/ppermute | solution.py:1094
  219.1 4.8 %copy-start.15 = (pred[256]{0:T(512)(128)(4,1)S(1)}, pred[256]{0:T(512)(128)(4,1)}, u32[]{:S(2)}) copy-start(pred[256]{0:T(512)(128)(4,1)} %copy-done.14) | copy-start | bytes 772
  219.1 4.7 %copy-start.18 = (f32[8]{0:T(128)S(1)}, f32[8]{0:T(128)}, u32[]{:S(2)}) copy-start(f32[8]{0:T(128)} %copy-done.17) | copy-start | bytes 100
  219.2 6.4 %copy-start.10 = (f32[4,5120]{1,0:T(4,128)S(1)}, f32[4,5120]{1,0:T(4,128)}, u32[]{:S(2)}) copy-start(f32[4,5120]{1,0:T(4,128)} %get-tuple-element.102) | copy-start | bytes 245764
  219.2 6.6 %copy-start.4 = (bf16[256,1024]{1,0:T(8,128)(2,1)S(1)}, bf16[256,1024]{1,0:T(8,128)(2,1)}, u32[]{:S(2)}) copy-start(bf16[256,1024]{1,0:T(8,128)(2,1)} %copy-done.2) | copy-start | bytes 1572868
  242.1 0.6 copy-start.20
  400.9 9.2 %copy-start.6 = (f32[2,7,32,768]{3,2,1,0:T(8,128)S(1)}, f32[2,7,32,768]{3,2,1,0:T(8,128)}, u32[]{:S(2)}) copy-start(f32[2,7,32,768]{3,2,1,0:T(8,128)} %get-tuple-element.107) | copy-start | bytes 4128772
  403.1 7.2 %copy-start.5 = (f32[32,8,640]{2,1,0:T(8,128)}, f32[32,8,640]{2,1,0:T(8,128)S(1)}, u32[]{:S(2)}) copy-start(f32[32,8,640]{2,1,0:T(8,128)S(1)} %reshape_reshape.4) | copy-start | bytes 1966084
  410.3 2.1 slice-start
  411.0 7.2 %copy-start.1 = (bf16[1024,1024]{1,0:T(8,128)(2,1)S(1)}, bf16[1024,1024]{1,0:T(8,128)(2,1)}, u32[]{:S(2)}) copy-start(bf16[1024,1024]{1,0:T(8,128)(2,1)} %param.36) | copy-start | bytes 6291460
